TPU v7x, 32 devices: a whole 2x2x4 slice. The times are simulated.
32 devices in a mesh: depth: 4 (over z), height: 8 (over y, x, core).
Axes of the slice: x: 2, y: 2, z: 4, core: 2. Of those that a mesh axis runs over, the one named last changes fastest.
Arguments:
- density: float32 [32, 512, 128], P('depth', 'height'), may hold values from -6 to 6
- light_vector: float32 [3], replicated, may hold values from -1 to 1
- colour_gain: float32 [3], replicated, may hold values from 0.5 to 3
- colour_bias: float32 [3], replicated, may hold values from -1 to 1
- shear_step: int32 [4], replicated, may hold values from 0 to 32
- reverse_view: int32 [4], replicated, may hold values from 0 to 1
Outputs:
- images: float32 [4, 4, 512, 128], P(None, None, ('height', 'depth'))
All inputs are finite; a program needn't handle non-finite values.
Results may differ from a plain program's by a relative error of at most 0.0003.
Values sent between devices are 32-bit elements; how exact they have to be, the bound alone decides.
A program may use at most 64 MiB of HBM per device.

v0:
```python
import functools

import jax
import jax.numpy as jnp
from jax import lax
from jax.experimental import pallas as pl
from jax.experimental.pallas import tpu as pltpu
from jax.sharding import PartitionSpec as P

EXTINCTION = 2.5
LEAD = 8
TOGETHER = 6
MESH = pl.DeviceIdType.MESH


def spans(low, high, size):
    return [(at, min(size, high - at)) for at in range(low, high, size)]


def line_kernel(
    towers,
    density,
    light_in,
    gain_in,
    bias_in,
    shear_in,
    reverse_in,
    out,
    light,
    gain,
    bias,
    shear,
    reverse,
    volume,
    fields,
    outgoing,
    incoming,
    handed,
    sent_sem,
    halo_sem,
    hand_sem,
    part_sem,
):
    planes, rows, cols = density.shape
    margin = rows // 2
    views = shear.shape[0]
    groups = 4
    share = rows // groups
    total_planes = planes * groups
    extinction = EXTINCTION / total_planes
    d = lax.axis_index("depth")
    h = lax.axis_index("height")
    above, below = (h - 1 >= 0) & (h - 1 < towers), (h + 1 >= 0) & (h + 1 < towers)
    end = LEAD + rows
    own_planes = pl.ds(2, planes)
    images, plane_sent, edge_sent, down_sent, up_sent, relay_sent = range(6)
    pair_in, peer_in, edge_in, down_in, up_in, relay_in = range(6)

    own = pltpu.make_async_copy(
        density, volume.at[own_planes, pl.ds(LEAD, rows)], sent_sem.at[images]
    )
    own.start()
    scalars = [
        pltpu.make_async_copy(source, target, sent_sem.at[1 + index])
        for index, (source, target) in enumerate(
            zip((light_in, gain_in, bias_in, shear_in, reverse_in), (light, gain, bias, shear, reverse))
        )
    ]
    for scalar in scalars:
        scalar.start()

    barrier = pltpu.get_barrier_semaphore()
    expected = jnp.int32(0)
    for step_d, step_h in ((1, 0), (-1, 0), (0, 1), (0, -1)):
        at, count = (d + step_d, groups) if step_d else (h + step_h, towers)
        ok = (at >= 0) & (at < count)
        expected = expected + jnp.where(ok, 1, 0)

        @pl.when(ok)
        def _(target=(d + step_d, h + step_h)):
            pl.semaphore_signal(barrier, inc=1, device_id=target, device_id_type=MESH)

    for scalar in scalars:
        scalar.wait()
    own.wait()

    lz, ly, lx = light[0], light[1], light[2]
    half_gain = [0.5 * gain[c] for c in range(3)]
    half_bias = [0.5 * bias[c] for c in range(3)]
    inside = jnp.where(below, 1.0, 0.0)

    def shade(plane, row, count, keep):
        at = LEAD + row
        centre = volume[plane, at : at + count]
        lane = lax.broadcasted_iota(jnp.int32, (count, cols), 1)
        following = jnp.where(lane == cols - 1, 0.0, pltpu.roll(centre, cols - 1, 1))
        previous = jnp.where(lane == 0, 0.0, pltpu.roll(centre, 1, 1))
        dx = following - previous
        dz = volume[plane + 1, at : at + count] - volume[plane - 1, at : at + count]
        dy = volume[plane, at + 1 : at + 1 + count] - volume[plane, at - 1 : at - 1 + count]
        facing = (lz * dz + ly * dy + lx * dx) * lax.rsqrt(4.0 + dz * dz + dy * dy + dx * dx)
        shading = 0.25 + 1.5 * jnp.maximum(facing, 0.0)
        optical = extinction * (
            jnp.maximum(centre, 0.0) + jnp.log1p(jnp.exp(-jnp.abs(centre)))
        )
        opacity = jnp.tanh(0.5 * optical) * (1.0 + jnp.exp(-optical))
        if keep is not None:
            opacity = opacity * keep
        lit = 0.5 * (opacity * shading)
        to = pl.ds(row, count)
        for c in range(3):
            fields[c, plane, to] = lit + lit * jnp.tanh(half_gain[c] * centre + half_bias[c])
        fields[3, plane, to] = opacity

    def shade_box(low, high, top, bottom):
        tiles = (bottom - top) // 8
        together = max(1, min(high - low, -(-TOGETHER // tiles)))
        looped = (high - low) // together if high - low > together else 0

        def some(plane, count):
            for step in range(count):
                for row, size in spans(top, min(bottom, rows), 16):
                    shade(plane + step, row, size, None)
                for row, size in spans(max(top, rows), bottom, 16):
                    shade(plane + step, row, size, inside)

        if looped:

            def step(index, _):
                some(low + index * together, together)
                return 0

            lax.fori_loop(0, looped, step, 0)
        done = low + looped * together
        if done < high:
            some(done, high - done)

    def copy_to(source, target, sent, received, device):
        return pltpu.make_async_remote_copy(
            src_ref=source,
            dst_ref=target,
            send_sem=sent_sem.at[sent],
            recv_sem=received,
            device_id=device,
            device_id_type=MESH,
        )

    def over(first, second, swap):
        front = [jnp.where(swap, b, a) for a, b in zip(first, second)]
        behind = [jnp.where(swap, a, b) for a, b in zip(first, second)]
        clear = 1.0 - front[3]
        return [f + clear * b for f, b in zip(front, behind)]

    everything = (0, share)

    def load(ref, block, view, part):
        return [ref[block, view, c, pl.ds(*part)] for c in range(4)]

    def store(ref, block, view, part, image):
        for c in range(4):
            ref[block, view, c, pl.ds(*part)] = image[c]

    def each_view(body):
        def step(view, _):
            body(view)
            return 0

        lax.fori_loop(0, views, step, 0)

    def brick(at):
        outer = at in (0, groups - 1)
        lower = at < groups // 2
        mate = at ^ 1
        first = at * planes - 2
        low = {0: 2, 1: 1, 2: 2, 3: 3}[at]
        high = {0: planes + 1, 1: planes + 2, 2: planes + 3, 3: planes + 2}[at]
        reach = (first + high - 1) * margin // total_planes
        extra = -(-reach // 8) * 8
        border = min(margin, -(-(reach + 1) // 8) * 8)
        mate_pair = pl.ds(0, 2) if lower else pl.ds(planes + 2, 2)
        peer_plane = pl.ds(planes + 2, 1) if lower else pl.ds(1, 1)
        edge = {0: planes + 1, 1: 1, 2: planes + 2, 3: 2}[at]
        mate_edge = {0: 1, 3: planes + 2}.get(at, edge)
        others = [2, 3] if lower else [0, 1]
        other = {0: 2, 1: 2, 2: 1, 3: 1}[at]
        peer = {1: 2, 2: 1}.get(at)
        halves = [(share // 2, share // 2), (0, share // 2)]
        parts = {0: halves, 1: [everything], 2: [everything], 3: [everything]}
        hand_at = {
            (block, part): index
            for index, (block, part) in enumerate((block, part) for block in others for part in parts[block])
        }

        def pair_copy():
            source = pl.ds(planes, 2) if lower else pl.ds(2, 2)
            return copy_to(
                volume.at[source, pl.ds(LEAD, rows)],
                volume.at[mate_pair, pl.ds(LEAD, rows)],
                plane_sent,
                halo_sem.at[pair_in],
                (mate, h),
            )

        def peer_copy():
            source = pl.ds(planes + 1, 1) if lower else pl.ds(2, 1)
            target = pl.ds(1, 1) if lower else pl.ds(planes + 2, 1)
            return copy_to(
                volume.at[source, pl.ds(LEAD, rows)],
                volume.at[target, pl.ds(LEAD, rows)],
                plane_sent,
                halo_sem.at[peer_in],
                (peer, h),
            )

        def edge_copy():
            return copy_to(
                volume.at[edge, pl.ds(0, LEAD)],
                volume.at[mate_edge, pl.ds(0, LEAD)],
                edge_sent,
                halo_sem.at[edge_in],
                (mate, h),
            )

        def down_copy(step):
            return copy_to(
                volume.at[own_planes, pl.ds(rows, LEAD)],
                volume.at[own_planes, pl.ds(0, LEAD)],
                down_sent,
                halo_sem.at[down_in],
                (d, h + step),
            )

        def up_copy(step):
            return copy_to(
                volume.at[own_planes, pl.ds(LEAD, border)],
                volume.at[own_planes, pl.ds(end, border)],
                up_sent,
                halo_sem.at[up_in],
                (d, h + step),
            )

        def relay_copy(which, step):
            return copy_to(
                volume.at[which, pl.ds(LEAD, border)],
                volume.at[which, pl.ds(end, border)],
                relay_sent,
                halo_sem.at[relay_in],
                (d, h + step),
            )

        relayed = pl.ds(0, 3)

        def hand(view, block, part):
            index = hand_at[block, part] * views + view
            return copy_to(
                outgoing.at[block, view, :, pl.ds(*part)],
                handed.at[block, view, :, pl.ds(*part)],
                images,
                hand_sem.at[index],
                (mate, h),
            )

        def send(view, block, part):
            slot = 0 if block == mate else views
            return copy_to(
                outgoing.at[block, view, :, pl.ds(*part)],
                incoming.at[at, view, :, pl.ds(*part)],
                images,
                part_sem.at[slot + view],
                (block, h),
            )

        def receive(view, source):
            slot = 0 if source == mate else views
            return copy_to(
                outgoing.at[at, view],
                incoming.at[source, view],
                images,
                part_sem.at[slot + view],
                (source, h),
            )

        def partial(view, block, part):
            step = shear[view]
            backward = reverse[view]
            count = high - low
            size = part[1]
            colour = [jnp.zeros((size, cols), jnp.float32) for _ in range(3)]
            clear = jnp.ones((size, cols), jnp.float32)
            covered = jnp.zeros((size, cols), jnp.float32)
            for i in range(count):
                plane = jnp.where(backward == 1, low + count - 1 - i, low + i)
                offset = lax.div((first + plane) * step, jnp.int32(total_planes))
                offset = jnp.minimum(jnp.maximum(offset, 0), reach)
                rows_at = pl.ds(offset + block * share + part[0], size)
                for c in range(3):
                    colour[c] = colour[c] + clear * fields[c, plane, rows_at]
                covered = covered + clear * fields[3, plane, rows_at]
                clear = 1.0 - covered
            return colour + [covered]

        def send_mate():
            def one(view):
                store(outgoing, mate, view, everything, partial(view, mate, everything))
                send(view, mate, everything).start()

            each_view(one)

        def keep_own():
            each_view(lambda view: store(incoming, at, view, everything, partial(view, at, everything)))

        def hand_over(block, part=everything):
            def one(view):
                store(outgoing, block, view, part, partial(view, block, part))
                hand(view, block, part).start()

            each_view(one)

        def pass_on(block, part=everything):
            def one(view):
                mine = partial(view, block, part)
                hand(view, block, part).wait_recv()
                theirs = load(handed, block, view, part)
                swap = reverse[view] == 1
                merged = over(theirs, mine, swap) if lower else over(mine, theirs, swap)
                store(outgoing, block, view, part, merged)
                send(view, block, part).start()

            each_view(one)

        def begin():
            with jax.named_scope("barrier"):
                pl.semaphore_wait(barrier, expected)
            if outer:
                pair_copy().start()
            else:
                peer_copy().start()

            @pl.when(below)
            def _():
                down_copy(1).start()

            @pl.when(above)
            def _():
                up_copy(-1).start()

        def blank():
            if outer:
                volume[1 if lower else planes + 2] = jnp.zeros(volume.shape[1:], jnp.float32)

            @pl.when(jnp.logical_not(above))
            def _():
                volume[:, :LEAD] = jnp.zeros((planes + 4, LEAD, cols), jnp.float32)

            @pl.when(jnp.logical_not(below))
            def _():
                volume[:, end : end + border] = jnp.zeros((planes + 4, border, cols), jnp.float32)

        def top_landed():
            @pl.when(above)
            def _():
                with jax.named_scope("w_down"):
                    down_copy(-1).wait_recv()

        def bottom_landed():
            @pl.when(below)
            def _():
                with jax.named_scope("w_up"):
                    up_copy(1).wait_recv()

        def edge_landed():
            @pl.when(above)
            def _():
                with jax.named_scope("w_edge"):
                    edge_copy().wait_recv()

        def edge_pass():
            @pl.when(above)
            def _():
                edge_copy().start()

        def relay(which):
            @pl.when(above)
            def _():
                relay_copy(which, -1).start()

        def relay_landed():
            @pl.when(below)
            def _():
                with jax.named_scope("w_relay"):
                    relay_copy(relayed, 1).wait_recv()

        blank()
        if at == 0:
            shade_box(low, high, LEAD, rows - LEAD)
            begin()
            with jax.named_scope("hand2"):
                hand_over(2)
            top_landed()
            edge_pass()
            bottom_landed()
            shade_box(low, high, rows - LEAD, rows + extra)
            with jax.named_scope("hand3"):
                hand_over(3)
            shade_box(low, high, 0, LEAD)
            with jax.named_scope("mate"):
                send_mate()
            keep_own()
        elif at == 3:
            begin()
            shade_box(low, high, LEAD, rows - LEAD)
            with jax.named_scope("hand0b"):
                hand_over(0, halves[0])
            top_landed()
            edge_pass()
            shade_box(low, high, 0, LEAD)
            with jax.named_scope("hand0a"):
                hand_over(0, halves[1])
            bottom_landed()
            shade_box(low, high, rows - LEAD, rows)
            with jax.named_scope("hand1"):
                hand_over(1)
            shade_box(low, high, rows, rows + extra)
            with jax.named_scope("mate"):
                send_mate()
            keep_own()
        else:
            shade_box(3, planes + 1, LEAD, rows - LEAD)
            begin()
            far_edge = planes + 1 if lower else 2
            seam = min(2 if lower else planes + 1, edge)

            def planes_in():
                with jax.named_scope("w_peer"):
                    peer_copy().wait_recv()
                relay(peer_plane)
                shade_box(far_edge, far_edge + 1, LEAD, rows - LEAD)
                with jax.named_scope("w_pair"):
                    pair_copy().wait_recv()
                relay(mate_pair)
                shade_box(seam, seam + 2, LEAD, rows - LEAD)

            def rim():
                top_landed()
                edge_landed()
                shade_box(low, high, 0, LEAD)

            def fringe():
                relay_landed()
                shade_box(seam, seam + 2, rows - LEAD, rows + extra)
                shade_box(far_edge, far_edge + 1, rows - LEAD, rows + extra)

            def bottom():
                bottom_landed()
                shade_box(3, planes + 1, rows - LEAD, rows + extra)

            if lower:
                bottom()
                planes_in()
                shade_box(far_edge, far_edge + 1, rows - LEAD, rows)
                with jax.named_scope("pass2"):
                    pass_on(2)
                rim()
                with jax.named_scope("mate"):
                    send_mate()
                fringe()
                with jax.named_scope("pass3"):
                    pass_on(3)
            else:
                planes_in()
                with jax.named_scope("pass0b"):
                    pass_on(0, halves[0])
                rim()
                with jax.named_scope("pass0a"):
                    pass_on(0, halves[1])
                bottom()
                fringe()
                with jax.named_scope("mate"):
                    send_mate()
                with jax.named_scope("pass1"):
                    pass_on(1)
            keep_own()

        def finish(view):
            swap = reverse[view] == 1
            with jax.named_scope("w_mate"):
                receive(view, mate).wait_recv()
            mine, theirs = (load(incoming, source, view, everything) for source in (at, mate))
            near = over(mine, theirs, swap) if at < mate else over(theirs, mine, swap)
            with jax.named_scope("w_other"):
                receive(view, other).wait_recv()
            far = load(incoming, other, view, everything)
            total = over(near, far, swap) if lower else over(far, near, swap)
            for c in range(4):
                out[c, view] = total[c]

        for view in range(views):
            finish(view)

        if outer:
            pair_copy().wait_send()

            @pl.when(above)
            def _():
                edge_copy().wait_send()
        else:
            peer_copy().wait_send()

            @pl.when(above)
            def _():
                relay_copy(relayed, -1).wait_send()

        @pl.when(below)
        def _():
            down_copy(1).wait_send()

        @pl.when(above)
        def _():
            up_copy(-1).wait_send()

        gone = pl.ds(0, groups - 1)
        copy_to(outgoing.at[gone], handed.at[gone], images, hand_sem.at[0], (mate, h)).wait_send()

    for at in range(groups):

        @pl.when(d == at)
        def _():
            brick(at)


def kernel(
    groups,
    towers,
    density,
    light,
    gain,
    bias,
    shear,
    reverse,
    out,
    volume,
    fields,
    outgoing,
    incoming,
    handed,
    local_sem,
    halo_send,
    halo_recv,
    hand_send,
    hand_recv,
    part_send,
    part_recv,
):
    planes, rows, cols = density.shape
    margin = rows // 2
    views = shear.shape[0]
    share = rows // groups
    total_planes = planes * groups
    extinction = EXTINCTION / total_planes
    d = lax.axis_index("depth")
    h = lax.axis_index("height")
    end = LEAD + rows
    tall = end + margin

    own = pltpu.make_async_copy(
        density, volume.at[pl.ds(1, planes), pl.ds(LEAD, rows)], local_sem
    )
    own.start()

    def near(step_d, step_h):
        ok = None
        for at, step, count in ((d, step_d, groups), (h, step_h, towers)):
            if step:
                test = (at + step >= 0) & (at + step < count)
                ok = test if ok is None else ok & test
        return ok, (d + step_d, h + step_h)

    barrier = pltpu.get_barrier_semaphore()
    beside = [(0, 1), (0, -1), (1, 1), (1, -1), (-1, 1), (-1, -1), (1, 0), (-1, 0)]
    if groups > 4:
        beside += [(step * hop, 0) for hop in range(2, groups) for step in (1, -1)]
    expected = jnp.int32(0)
    for step_d, step_h in beside:
        ok, target = near(step_d, step_h)
        expected = expected + jnp.where(ok, 1, 0)

        @pl.when(ok)
        def _(target=target):
            pl.semaphore_signal(barrier, inc=1, device_id=target, device_id_type=MESH)

    pl.semaphore_wait(barrier, expected)

    whole = pl.ds(0, planes)
    inner = pl.ds(1, planes)
    first, last = pl.ds(0, 1), pl.ds(planes - 1, 1)
    low, high = pl.ds(0, 1), pl.ds(planes + 1, 1)
    routes = [
        ((1, 0), last, (0, rows), low, LEAD),
        ((-1, 0), first, (0, rows), high, LEAD),
        ((0, 1), whole, (rows - LEAD, LEAD), inner, 0),
        ((0, -1), whole, (0, margin), inner, end),
        ((1, -1), last, (0, margin), low, end),
        ((-1, -1), first, (0, margin), high, end),
    ]

    def halo(index, reach):
        step, from_planes, (row, count), to_planes, to_row = routes[index]
        return pltpu.make_async_remote_copy(
            src_ref=density.at[from_planes, pl.ds(row, count)],
            dst_ref=volume.at[to_planes, pl.ds(to_row, count)],
            send_sem=halo_send.at[index],
            recv_sem=halo_recv.at[index],
            device_id=reach,
            device_id_type=MESH,
        )

    for index, route in enumerate(routes):
        ok, target = near(*route[0])

        @pl.when(ok)
        def _(index=index, target=target):
            halo(index, target).start()

    @pl.when(d == 0)
    def _():
        volume[0] = jnp.zeros(volume.shape[1:], jnp.float32)

    @pl.when(d == groups - 1)
    def _():
        volume[planes + 1] = jnp.zeros(volume.shape[1:], jnp.float32)

    @pl.when(h == 0)
    def _():
        volume[1 : planes + 1, :LEAD] = jnp.zeros((planes, LEAD, cols), jnp.float32)

    @pl.when(h == towers - 1)
    def _():
        volume[:, end:tall] = jnp.zeros((planes + 2, margin, cols), jnp.float32)

    own.wait()

    lz, ly, lx = light[0], light[1], light[2]
    half_gain = [0.5 * gain[c] for c in range(3)]
    half_bias = [0.5 * bias[c] for c in range(3)]

    def shade(plane, row, count, keep):
        at = LEAD + row
        centre = volume[plane, at : at + count]
        lane = lax.broadcasted_iota(jnp.int32, (count, cols), 1)
        following = jnp.where(lane == cols - 1, 0.0, pltpu.roll(centre, cols - 1, 1))
        previous = jnp.where(lane == 0, 0.0, pltpu.roll(centre, 1, 1))
        dx = following - previous
        dz = volume[plane + 1, at : at + count] - volume[plane - 1, at : at + count]
        dy = volume[plane, at + 1 : at + 1 + count] - volume[plane, at - 1 : at - 1 + count]
        facing = (lz * dz + ly * dy + lx * dx) * lax.rsqrt(4.0 + dz * dz + dy * dy + dx * dx)
        shading = 0.25 + 1.5 * jnp.maximum(facing, 0.0)
        optical = extinction * (
            jnp.maximum(centre, 0.0) + jnp.log1p(jnp.exp(-jnp.abs(centre)))
        )
        opacity = jnp.tanh(0.5 * optical) * (1.0 + jnp.exp(-optical))
        if keep is not None:
            opacity = opacity * keep
        lit = 0.5 * (opacity * shading)
        to = pl.ds(row, count)
        for c in range(3):
            fields[c, plane - 1, to] = lit + lit * jnp.tanh(half_gain[c] * centre + half_bias[c])
        fields[3, plane - 1, to] = opacity

    inside = jnp.where(h < towers - 1, 1.0, 0.0)

    def early(plane, _):
        for row, count in spans(LEAD, rows - LEAD, 16):
            shade(plane, row, count, None)
        return 0

    lax.fori_loop(2, planes, early, 0)

    def landed(index):
        step_d, step_h = routes[index][0]
        ok, source = near(-step_d, -step_h)

        @pl.when(ok)
        def _():
            halo(index, source).wait_recv()

    def shade_low():
        for index in (0, 1, 2):
            landed(index)
        for plane in range(1, planes + 1):
            shade(plane, 0, LEAD, None)
        for row, count in spans(LEAD, rows - LEAD, 16):
            for plane in (1, planes):
                shade(plane, row, count, None)

    def shade_high():
        for index in (3, 4, 5):
            landed(index)

        def bottom(at, _):
            for plane in (2 * at + 1, 2 * at + 2):
                shade(plane, rows - LEAD, LEAD, None)
                for row, count in spans(rows, rows + margin, 16):
                    shade(plane, row, count, inside)
            return 0

        lax.fori_loop(0, planes // 2, bottom, 0)

    first_plane = d * planes

    def partial(view, block):
        step = shear[view]
        backward = reverse[view]
        colour = [jnp.zeros((share, cols), jnp.float32) for _ in range(3)]
        clear = jnp.ones((share, cols), jnp.float32)
        covered = jnp.zeros((share, cols), jnp.float32)
        for i in range(planes):
            plane = i + backward * (planes - 1 - 2 * i)
            offset = lax.div((first_plane + plane) * step, jnp.int32(total_planes))
            at = pl.ds(offset + block * share, share)
            for c in range(3):
                colour[c] = colour[c] + clear * fields[c, plane, at]
            covered = covered + clear * fields[3, plane, at]
            clear = 1.0 - covered
        return colour + [covered]

    odd = lax.rem(d, 2)
    out_step = 2 * odd - 1
    mate = d - out_step
    pair = lax.div(d, 2)
    beyond = odd * (groups - 1 - d) + (1 - odd) * d
    handing = odd * (d - 1) + (1 - odd) * (groups - 2 - d)

    def over(first, second, swap):
        front = [jnp.where(swap, b, a) for a, b in zip(first, second)]
        behind = [jnp.where(swap, a, b) for a, b in zip(first, second)]
        clear = 1.0 - front[3]
        return [f + clear * b for f, b in zip(front, behind)]

    def load(ref, block, view):
        return [ref[block, view, c] for c in range(4)]

    def store(ref, block, view, image):
        for c in range(4):
            ref[block, view, c] = image[c]

    def hand(view, block):
        return pltpu.make_async_remote_copy(
            src_ref=outgoing.at[block, view],
            dst_ref=handed.at[block, view],
            send_sem=hand_send.at[view, block],
            recv_sem=hand_recv.at[view, block],
            device_id=(mate, h),
            device_id_type=MESH,
        )

    def send(view, block):
        return pltpu.make_async_remote_copy(
            src_ref=outgoing.at[block, view],
            dst_ref=incoming.at[d, view],
            send_sem=part_send.at[view, block],
            recv_sem=part_recv.at[view, d],
            device_id=(block, h),
            device_id_type=MESH,
        )

    def receive(view, source):
        return pltpu.make_async_remote_copy(
            src_ref=outgoing.at[source, view],
            dst_ref=incoming.at[source, view],
            send_sem=part_send.at[view, source],
            recv_sem=part_recv.at[view, source],
            device_id=(source, h),
            device_id_type=MESH,
        )

    def each(count, body):
        def step(k, _):
            body(k)
            return 0

        lax.fori_loop(0, count, step, 0)

    def hand_over(view, k):
        block = odd * k + (1 - odd) * (groups - 1 - k)
        store(outgoing, block, view, partial(view, block))
        hand(view, block).start()

    def prepare(view, k):
        block = d + out_step * (1 + k)
        store(outgoing, block, view, partial(view, block))

    def to_mate(view):
        store(outgoing, mate, view, partial(view, mate))
        send(view, mate).start()

    def pass_on(view, k):
        block = odd * (groups - 1 - k) + (1 - odd) * k
        hand(view, block).wait_recv()
        own_part, other = load(outgoing, block, view), load(handed, block, view)
        swap = reverse[view] != odd
        store(outgoing, block, view, over(own_part, other, swap))
        send(view, block).start()

    reach = lax.div((first_plane + planes - 1) * margin, jnp.int32(total_planes))

    def hand_round(early):
        def one(k):
            block = odd * k + (1 - odd) * (groups - 1 - k)
            ready = ((block + 1) * share + reach <= rows - LEAD) & (odd == 1)

            @pl.when(ready if early else jnp.logical_not(ready))
            def _():
                each(views, lambda view: hand_over(view, k))

        each(handing, one)

    shade_low()
    hand_round(True)
    shade_high()
    hand_round(False)
    each(views, to_mate)
    each(views, lambda view: each(beyond, lambda k: prepare(view, k)))
    each(views, lambda view: store(incoming, d, view, partial(view, d)))
    each(beyond, lambda k: each(views, lambda view: pass_on(view, k)))

    def finish(view):
        swap = reverse[view] == 1
        receive(view, mate).wait_recv()
        both = over(load(incoming, d, view), load(incoming, mate, view), reverse[view] != odd)
        store(incoming, 2 * pair + 1, view, both)
        sources = [jnp.where(j > pair, 2 * j, 2 * j + 1) for j in range(groups // 2)]
        for j, source in enumerate(sources):

            @pl.when(j != pair)
            def _():
                receive(view, source).wait_recv()

        total = load(incoming, sources[0], view)
        for source in sources[1:]:
            total = over(total, load(incoming, source, view), swap)
        for c in range(4):
            out[c, view] = total[c]

    for view in range(views):
        finish(view)

    for index, route in enumerate(routes):
        ok, target = near(*route[0])

        @pl.when(ok)
        def _(index=index, target=target):
            halo(index, target).wait_send()

    def sent(view):
        send(view, mate).wait_send()
        each(handing, lambda k: hand(view, d - out_step * (2 + k)).wait_send())
        each(beyond, lambda k: send(view, d + out_step * (1 + k)).wait_send())

    each(views, sent)


def general(groups, towers, density, light, gain, bias, shear, reverse):
    planes, rows, cols = density.shape
    views = shear.shape[0]
    share = rows // groups
    tall = LEAD + rows + rows // 2
    scalars = pl.BlockSpec(memory_space=pltpu.SMEM)
    return pl.pallas_call(
        functools.partial(kernel, groups, towers),
        name="render",
        out_shape=pltpu.VMEM((4, views, share, cols), jnp.float32),
        in_specs=[pl.BlockSpec(memory_space=pltpu.HBM)] + [scalars] * 5,
        out_specs=pl.BlockSpec(memory_space=pltpu.VMEM),
        scratch_shapes=[
            pltpu.VMEM((planes + 2, tall + LEAD, cols), jnp.float32),
            pltpu.VMEM((4, planes, rows + rows // 2, cols), jnp.float32),
            pltpu.VMEM((groups, views, 4, share, cols), jnp.float32),
            pltpu.VMEM((groups, views, 4, share, cols), jnp.float32),
            pltpu.VMEM((groups, views, 4, share, cols), jnp.float32),
            pltpu.SemaphoreType.DMA,
            pltpu.SemaphoreType.DMA((6,)),
            pltpu.SemaphoreType.DMA((6,)),
            pltpu.SemaphoreType.DMA((views, groups)),
            pltpu.SemaphoreType.DMA((views, groups)),
            pltpu.SemaphoreType.DMA((views, groups)),
            pltpu.SemaphoreType.DMA((views, groups)),
        ],
        compiler_params=pltpu.CompilerParams(collective_id=0, has_side_effects=True, vmem_limit_bytes=60 * 1024 * 1024),
    )(density, light, gain, bias, shear, reverse)


def line(towers, density, light, gain, bias, shear, reverse):
    planes, rows, cols = density.shape
    views = shear.shape[0]
    groups = 4
    share = rows // groups
    whole = pl.BlockSpec(memory_space=pltpu.HBM)
    images = pltpu.VMEM((groups, views, 4, share, cols), jnp.float32)
    return pl.pallas_call(
        functools.partial(line_kernel, towers),
        name="render",
        out_shape=pltpu.VMEM((4, views, share, cols), jnp.float32),
        in_specs=[whole] * 6,
        out_specs=pl.BlockSpec(memory_space=pltpu.VMEM),
        scratch_shapes=[pltpu.SMEM(scalar.shape, scalar.dtype) for scalar in (light, gain, bias, shear, reverse)]
        + [
            pltpu.VMEM((planes + 4, LEAD + rows + rows // 2 + LEAD, cols), jnp.float32),
            pltpu.VMEM((4, planes + 4, rows + rows // 2, cols), jnp.float32),
            images,
            images,
            images,
            pltpu.SemaphoreType.DMA((6,)),
            pltpu.SemaphoreType.DMA((6,)),
            pltpu.SemaphoreType.DMA((3 * views,)),
            pltpu.SemaphoreType.DMA((2 * views,)),
        ],
        compiler_params=pltpu.CompilerParams(collective_id=0, has_side_effects=True, vmem_limit_bytes=60 * 1024 * 1024),
    )(density, light, gain, bias, shear, reverse)


def on_device(groups, towers, density, light, gain, bias, shear, reverse):
    planes, rows, _ = density.shape
    if groups == 4 and planes >= 8 and rows % 64 == 0:
        return line(towers, density, light, gain, bias, shear, reverse)
    return general(groups, towers, density, light, gain, bias, shear, reverse)


def solution(mesh):
    groups, towers = mesh.shape["depth"], mesh.shape["height"]
    placed = (P("depth", "height", None), P(), P(), P(), P(), P())
    return jax.shard_map(
        functools.partial(on_device, groups, towers),
        mesh=mesh,
        in_specs=placed,
        out_specs=P(None, None, ("height", "depth"), None),
        check_vma=False,
    )
```

profile of v0, /device:TPU:0, one launch (start us, length us, event | category | flops | bytes accessed | tf_op | source)
XLA Modules:
  0.0 17.3 jit_solution(8409924636603937770)
XLA Ops:
  0.0 16.6 %render.1 = f32[4,4,16,128]{3,2,1,0:T(8,128)S(1)} custom-call(f32[8,64,128]{2,1,0:T(8,128)} %density.1, f32[3]{0:T(128)} %light_in.1, f32[3]{0:T(128)} %gain_in.1, f32[3]{0:T(128)} %bias_in.1, s32[4]{0:T(128)} %shear_in.1, s32[4]{0:T(128)} %reverse_in.1), custom_call_target="tpu_custom_call" | custom-call | tf_op jit(solution)/shard_map/render/pallas_call | solution.py:899
  16.6 0.7 %copy.8 = f32[4,4,16,128]{3,2,1,0:T(8,128)} copy(f32[4,4,16,128]{3,2,1,0:T(8,128)S(1)} %render.1) | data formatting | bytes 262144
where the time goes:
time: 17.5 us; the launch traced here: 17.3 us
  Pallas kernels  16.6 us (95%)
  local copies, waits for them, and re-layouts  0.66 us (4%)
    pallas_call x1, Pallas kernels, line(): pl.pallas_call(functools.partial(line_kernel, towers), name='render', out...  16.6 us
    unnamed x1, local copies, waits for them, and re-layouts  0.66 us

commit v1 on v0

--- a/solution.py
+++ b/solution.py
@@ -53,8 +53,8 @@
     above, below = (h - 1 >= 0) & (h - 1 < towers), (h + 1 >= 0) & (h + 1 < towers)
     end = LEAD + rows
     own_planes = pl.ds(2, planes)
-    images, plane_sent, edge_sent, down_sent, up_sent, relay_sent = range(6)
-    pair_in, peer_in, edge_in, down_in, up_in, relay_in = range(6)
+    images, plane_sent, edge_sent, down_sent, up_sent, corner_sent = range(6)
+    pair_in, peer_in, edge_in, down_in, up_in, pair_corner_in, peer_corner_in = range(7)
 
     own = pltpu.make_async_copy(
         density, volume.at[own_planes, pl.ds(LEAD, rows)], sent_sem.at[images]
@@ -69,16 +69,38 @@
     for scalar in scalars:
         scalar.start()
 
+    def valid(step_d, step_h):
+        ok = None
+        for at, step, count in ((d, step_d, groups), (h, step_h, towers)):
+            if step:
+                test = (at + step >= 0) & (at + step < count)
+                ok = test if ok is None else ok & test
+        return ok
+
     barrier = pltpu.get_barrier_semaphore()
     expected = jnp.int32(0)
-    for step_d, step_h in ((1, 0), (-1, 0), (0, 1), (0, -1)):
-        at, count = (d + step_d, groups) if step_d else (h + step_h, towers)
-        ok = (at >= 0) & (at < count)
-        expected = expected + jnp.where(ok, 1, 0)
-
-        @pl.when(ok)
-        def _(target=(d + step_d, h + step_h)):
-            pl.semaphore_signal(barrier, inc=1, device_id=target, device_id_type=MESH)
+    beside = [(1, 0), (-1, 0), (0, 1), (0, -1)]
+    greets = {at: list(beside) for at in range(groups)}
+    awaits = {at: list(beside) for at in range(groups)}
+    for at in (1, 2):
+        mate, peer = at ^ 1, 3 - at
+        for step_h in (1, -1):
+            greets[at].append((mate - at, step_h))
+            awaits[mate].append((at - mate, -step_h))
+        greets[at].append((peer - at, 1))
+        awaits[peer].append((at - peer, -1))
+    for at in range(groups):
+
+        for step in greets[at]:
+
+            @pl.when((d == at) & valid(*step))
+            def _(step=step):
+                pl.semaphore_signal(
+                    barrier, inc=1, device_id=(d + step[0], h + step[1]), device_id_type=MESH
+                )
+
+        for step in awaits[at]:
+            expected = expected + jnp.where((d == at) & valid(*step), 1, 0)
 
     for scalar in scalars:
         scalar.wait()
@@ -167,18 +189,20 @@
 
         lax.fori_loop(0, views, step, 0)
 
+    def extent(at):
+        low = {0: 2, 1: 1, 2: 2, 3: 3}[at]
+        high = {0: planes + 1, 1: planes + 2, 2: planes + 3, 3: planes + 2}[at]
+        reach = (at * planes + high - 3) * margin // total_planes
+        return low, high, reach, min(margin, -(-(reach + 1) // 8) * 8)
+
     def brick(at):
         outer = at in (0, groups - 1)
         lower = at < groups // 2
         mate = at ^ 1
         first = at * planes - 2
-        low = {0: 2, 1: 1, 2: 2, 3: 3}[at]
-        high = {0: planes + 1, 1: planes + 2, 2: planes + 3, 3: planes + 2}[at]
-        reach = (first + high - 1) * margin // total_planes
+        low, high, reach, border = extent(at)
         extra = -(-reach // 8) * 8
-        border = min(margin, -(-(reach + 1) // 8) * 8)
         mate_pair = pl.ds(0, 2) if lower else pl.ds(planes + 2, 2)
-        peer_plane = pl.ds(planes + 2, 1) if lower else pl.ds(1, 1)
         edge = {0: planes + 1, 1: 1, 2: planes + 2, 3: 2}[at]
         mate_edge = {0: 1, 3: planes + 2}.get(at, edge)
         others = [2, 3] if lower else [0, 1]
@@ -191,35 +215,39 @@
             for index, (block, part) in enumerate((block, part) for block in others for part in parts[block])
         }
 
+        def plane_copy(source, target, take, put, sent, received, device):
+            return copy_to(
+                volume.at[source, pl.ds(*take)],
+                volume.at[target, pl.ds(*put)],
+                sent,
+                halo_sem.at[received],
+                device,
+            )
+
+        own_pair = pl.ds(planes, 2) if lower else pl.ds(2, 2)
+        own_peer = pl.ds(planes + 1, 1) if lower else pl.ds(2, 1)
+        peer_target = pl.ds(1, 1) if lower else pl.ds(planes + 2, 1)
+        peer_border = extent(peer)[3] if peer else None
+        pair_border = extent(mate)[3] if outer else border
+        whole = (LEAD, rows)
+
         def pair_copy():
-            source = pl.ds(planes, 2) if lower else pl.ds(2, 2)
-            return copy_to(
-                volume.at[source, pl.ds(LEAD, rows)],
-                volume.at[mate_pair, pl.ds(LEAD, rows)],
-                plane_sent,
-                halo_sem.at[pair_in],
-                (mate, h),
-            )
+            return plane_copy(own_pair, mate_pair, whole, whole, plane_sent, pair_in, (mate, h))
 
         def peer_copy():
-            source = pl.ds(planes + 1, 1) if lower else pl.ds(2, 1)
-            target = pl.ds(1, 1) if lower else pl.ds(planes + 2, 1)
-            return copy_to(
-                volume.at[source, pl.ds(LEAD, rows)],
-                volume.at[target, pl.ds(LEAD, rows)],
-                plane_sent,
-                halo_sem.at[peer_in],
-                (peer, h),
-            )
-
-        def edge_copy():
-            return copy_to(
-                volume.at[edge, pl.ds(0, LEAD)],
-                volume.at[mate_edge, pl.ds(0, LEAD)],
-                edge_sent,
-                halo_sem.at[edge_in],
-                (mate, h),
-            )
+            return plane_copy(own_peer, peer_target, whole, whole, plane_sent, peer_in, (peer, h))
+
+        def pair_corner(step):
+            take, put = (LEAD, pair_border), (end, pair_border)
+            return plane_copy(own_pair, mate_pair, take, put, corner_sent, pair_corner_in, (d + mate - at, h + step))
+
+        def peer_corner(step, count):
+            take, put = (LEAD, count), (end, count)
+            return plane_copy(own_peer, peer_target, take, put, corner_sent, peer_corner_in, (d + peer - at, h + step))
+
+        def edge_copy(step):
+            take, put = (rows, LEAD), (0, LEAD)
+            return plane_copy(edge, mate_edge, take, put, edge_sent, edge_in, (d + mate - at, h + step))
 
         def down_copy(step):
             return copy_to(
@@ -238,17 +266,6 @@
                 halo_sem.at[up_in],
                 (d, h + step),
             )
-
-        def relay_copy(which, step):
-            return copy_to(
-                volume.at[which, pl.ds(LEAD, border)],
-                volume.at[which, pl.ds(end, border)],
-                relay_sent,
-                halo_sem.at[relay_in],
-                (d, h + step),
-            )
-
-        relayed = pl.ds(0, 3)
 
         def hand(view, block, part):
             index = hand_at[block, part] * views + view
@@ -339,9 +356,15 @@
             @pl.when(below)
             def _():
                 down_copy(1).start()
+                if outer:
+                    edge_copy(1).start()
 
             @pl.when(above)
             def _():
+                if outer:
+                    pair_corner(-1).start()
+                else:
+                    peer_corner(-1, peer_border).start()
                 up_copy(-1).start()
 
         def blank():
@@ -368,27 +391,18 @@
                 with jax.named_scope("w_up"):
                     up_copy(1).wait_recv()
 
+        def corners_landed():
+            @pl.when(below)
+            def _():
+                with jax.named_scope("w_corner"):
+                    peer_corner(1, border).wait_recv()
+                    pair_corner(1).wait_recv()
+
         def edge_landed():
             @pl.when(above)
             def _():
                 with jax.named_scope("w_edge"):
-                    edge_copy().wait_recv()
-
-        def edge_pass():
-            @pl.when(above)
-            def _():
-                edge_copy().start()
-
-        def relay(which):
-            @pl.when(above)
-            def _():
-                relay_copy(which, -1).start()
-
-        def relay_landed():
-            @pl.when(below)
-            def _():
-                with jax.named_scope("w_relay"):
-                    relay_copy(relayed, 1).wait_recv()
+                    edge_copy(-1).wait_recv()
 
         blank()
         if at == 0:
@@ -397,7 +411,6 @@
             with jax.named_scope("hand2"):
                 hand_over(2)
             top_landed()
-            edge_pass()
             bottom_landed()
             shade_box(low, high, rows - LEAD, rows + extra)
             with jax.named_scope("hand3"):
@@ -412,7 +425,6 @@
             with jax.named_scope("hand0b"):
                 hand_over(0, halves[0])
             top_landed()
-            edge_pass()
             shade_box(low, high, 0, LEAD)
             with jax.named_scope("hand0a"):
                 hand_over(0, halves[1])
@@ -430,53 +442,44 @@
             far_edge = planes + 1 if lower else 2
             seam = min(2 if lower else planes + 1, edge)
 
-            def planes_in():
-                with jax.named_scope("w_peer"):
-                    peer_copy().wait_recv()
-                relay(peer_plane)
-                shade_box(far_edge, far_edge + 1, LEAD, rows - LEAD)
-                with jax.named_scope("w_pair"):
-                    pair_copy().wait_recv()
-                relay(mate_pair)
-                shade_box(seam, seam + 2, LEAD, rows - LEAD)
+            top_landed()
+            shade_box(3, planes + 1, 0, LEAD)
+            bottom_landed()
+            shade_box(3, planes + 1, rows - LEAD, rows + extra)
+            with jax.named_scope("w_peer"):
+                peer_copy().wait_recv()
+            shade_box(far_edge, far_edge + 1, 0, rows)
+            with jax.named_scope("w_pair"):
+                pair_copy().wait_recv()
+            shade_box(seam, seam + 2, LEAD, rows - LEAD)
 
             def rim():
-                top_landed()
                 edge_landed()
-                shade_box(low, high, 0, LEAD)
+                shade_box(seam, seam + 2, 0, LEAD)
 
             def fringe():
-                relay_landed()
+                corners_landed()
                 shade_box(seam, seam + 2, rows - LEAD, rows + extra)
-                shade_box(far_edge, far_edge + 1, rows - LEAD, rows + extra)
-
-            def bottom():
-                bottom_landed()
-                shade_box(3, planes + 1, rows - LEAD, rows + extra)
+                shade_box(far_edge, far_edge + 1, rows, rows + extra)
 
             if lower:
-                bottom()
-                planes_in()
-                shade_box(far_edge, far_edge + 1, rows - LEAD, rows)
-                with jax.named_scope("pass2"):
-                    pass_on(2)
                 rim()
                 with jax.named_scope("mate"):
                     send_mate()
+                with jax.named_scope("pass2"):
+                    pass_on(2)
                 fringe()
                 with jax.named_scope("pass3"):
                     pass_on(3)
             else:
-                planes_in()
                 with jax.named_scope("pass0b"):
                     pass_on(0, halves[0])
                 rim()
-                with jax.named_scope("pass0a"):
-                    pass_on(0, halves[1])
-                bottom()
                 fringe()
                 with jax.named_scope("mate"):
                     send_mate()
+                with jax.named_scope("pass0a"):
+                    pass_on(0, halves[1])
                 with jax.named_scope("pass1"):
                     pass_on(1)
             keep_own()
@@ -499,24 +502,22 @@
 
         if outer:
             pair_copy().wait_send()
-
-            @pl.when(above)
-            def _():
-                edge_copy().wait_send()
         else:
             peer_copy().wait_send()
-
-            @pl.when(above)
-            def _():
-                relay_copy(relayed, -1).wait_send()
 
         @pl.when(below)
         def _():
             down_copy(1).wait_send()
+            if outer:
+                edge_copy(1).wait_send()
 
         @pl.when(above)
         def _():
             up_copy(-1).wait_send()
+            if outer:
+                pair_corner(-1).wait_send()
+            else:
+                peer_corner(-1, peer_border).wait_send()
 
         gone = pl.ds(0, groups - 1)
         copy_to(outgoing.at[gone], handed.at[gone], images, hand_sem.at[0], (mate, h)).wait_send()
@@ -910,7 +911,7 @@
             images,
             images,
             pltpu.SemaphoreType.DMA((6,)),
-            pltpu.SemaphoreType.DMA((6,)),
+            pltpu.SemaphoreType.DMA((7,)),
             pltpu.SemaphoreType.DMA((3 * views,)),
             pltpu.SemaphoreType.DMA((2 * views,)),
         ],

time: 17.5 us -> 16.8 us (0.960)
  Pallas kernels: 16.6 us -> 16 us
    pallas_call x1, Pallas kernels: 16.6 us -> 16 us  [line(): pl.pallas_call(functools.partial(line_kernel, towers), name='render', out...]
where the time goes in v1:
time: 16.8 us; the launch traced here: 16.7 us
  Pallas kernels  16 us (95%)
  local copies, waits for them, and re-layouts  0.66 us (4%)
    pallas_call x1, Pallas kernels, line(): pl.pallas_call(functools.partial(line_kernel, towers), name='render', out...  16 us
    unnamed x1, local copies, waits for them, and re-layouts  0.66 us

profile of v1, /device:TPU:0, one launch (start us, length us, event | category | flops | bytes accessed | tf_op | source)
XLA Modules:
  0.0 16.7 jit_solution(10624609776444705033)
XLA Ops:
  0.0 16.0 %render.1 = f32[4,4,16,128]{3,2,1,0:T(8,128)S(1)} custom-call(f32[8,64,128]{2,1,0:T(8,128)} %density.1, f32[3]{0:T(128)} %light_in.1, f32[3]{0:T(128)} %gain_in.1, f32[3]{0:T(128)} %bias_in.1, s32[4]{0:T(128)} %shear_in.1, s32[4]{0:T(128)} %reverse_in.1), custom_call_target="tpu_custom_call" | custom-call | tf_op jit(solution)/shard_map/render/pallas_call | solution.py:900
  16.0 0.7 %copy.8 = f32[4,4,16,128]{3,2,1,0:T(8,128)} copy(f32[4,4,16,128]{3,2,1,0:T(8,128)S(1)} %render.1) | data formatting | bytes 262144

commit v2 on v1

--- a/solution.py
+++ b/solution.py
@@ -53,8 +53,10 @@
     above, below = (h - 1 >= 0) & (h - 1 < towers), (h + 1 >= 0) & (h + 1 < towers)
     end = LEAD + rows
     own_planes = pl.ds(2, planes)
-    images, plane_sent, edge_sent, down_sent, up_sent, corner_sent = range(6)
-    pair_in, peer_in, edge_in, down_in, up_in, pair_corner_in, peer_corner_in = range(7)
+    images, plane_sent, edge_sent, down_sent, up_sent, corner_sent, rest_sent = range(7)
+    slab_sent, slab_edge_sent = edge_sent, rest_sent
+    pair_in, peer_in, edge_in, down_in, up_in, pair_corner_in, peer_corner_in, rest_in = range(8)
+    slab_in, slab_edge_in, slab_end_in = pair_in, edge_in, peer_in
 
     own = pltpu.make_async_copy(
         density, volume.at[own_planes, pl.ds(LEAD, rows)], sent_sem.at[images]
@@ -89,6 +91,9 @@
             awaits[mate].append((at - mate, -step_h))
         greets[at].append((peer - at, 1))
         awaits[peer].append((at - peer, -1))
+    for at, *step in ((0, 1, -1), (0, 2, 0)):
+        greets[at].append(tuple(step))
+        awaits[at + step[0]].append((-step[0], -step[1]))
     for at in range(groups):
 
         for step in greets[at]:
@@ -174,6 +179,8 @@
         return [f + clear * b for f, b in zip(front, behind)]
 
     everything = (0, share)
+    distant = (lax.rem(h, max(towers // 2, 1)) == 0) & (h > 0)
+    some, rest = (0, views // 2), (views // 2, views)
 
     def load(ref, block, view, part):
         return [ref[block, view, c, pl.ds(*part)] for c in range(4)]
@@ -182,12 +189,12 @@
         for c in range(4):
             ref[block, view, c, pl.ds(*part)] = image[c]
 
-    def each_view(body):
+    def each_view(body, start=0, stop=views):
         def step(view, _):
             body(view)
             return 0
 
-        lax.fori_loop(0, views, step, 0)
+        lax.fori_loop(start, stop, step, 0)
 
     def extent(at):
         low = {0: 2, 1: 1, 2: 2, 3: 3}[at]
@@ -231,8 +238,14 @@
         pair_border = extent(mate)[3] if outer else border
         whole = (LEAD, rows)
 
+        cut = rows - share
+        soon, after = ((LEAD + share, cut), (LEAD, share)) if lower else ((LEAD, cut), (LEAD + cut, share))
+
         def pair_copy():
-            return plane_copy(own_pair, mate_pair, whole, whole, plane_sent, pair_in, (mate, h))
+            return plane_copy(own_pair, mate_pair, soon, soon, plane_sent, pair_in, (mate, h))
+
+        def pair_rest():
+            return plane_copy(own_pair, mate_pair, after, after, rest_sent, rest_in, (mate, h))
 
         def peer_copy():
             return plane_copy(own_peer, peer_target, whole, whole, plane_sent, peer_in, (peer, h))
@@ -248,6 +261,24 @@
         def edge_copy(step):
             take, put = (rows, LEAD), (0, LEAD)
             return plane_copy(edge, mate_edge, take, put, edge_sent, edge_in, (d + mate - at, h + step))
+
+        span_high = 2 * planes + 2
+        span_reach = extent(1)[2]
+        span_rows = share + extent(1)[3]
+        slab = pl.ds(planes + 2, planes)
+        slab_end = pl.ds(2 * planes + 2, 1)
+
+        def slab_copy():
+            take = (LEAD, span_rows)
+            return plane_copy(own_planes, slab, take, take, slab_sent, slab_in, (0 if at else 1, h))
+
+        def slab_edge_copy(step):
+            take, put = (rows, LEAD), (0, LEAD)
+            return plane_copy(own_planes, slab, take, put, slab_edge_sent, slab_edge_in, (d + (-1 if at else 1), h + step))
+
+        def slab_end_copy():
+            take = (LEAD, span_rows)
+            return plane_copy(pl.ds(2, 1), slab_end, take, take, slab_sent, slab_end_in, (0 if at else 2, h))
 
         def down_copy(step):
             return copy_to(
@@ -297,7 +328,7 @@
                 (source, h),
             )
 
-        def partial(view, block, part):
+        def partial(view, block, part, high=high, reach=reach):
             step = shear[view]
             backward = reverse[view]
             count = high - low
@@ -324,16 +355,17 @@
             each_view(one)
 
         def keep_own():
-            each_view(lambda view: store(incoming, at, view, everything, partial(view, at, everything)))
-
-        def hand_over(block, part=everything):
+            span = (span_high, span_reach) if at == 0 else (high, reach)
+            each_view(lambda view: store(incoming, at, view, everything, partial(view, at, everything, *span)))
+
+        def hand_over(block, part=everything, which=(0, views)):
             def one(view):
                 store(outgoing, block, view, part, partial(view, block, part))
                 hand(view, block, part).start()
 
-            each_view(one)
-
-        def pass_on(block, part=everything):
+            each_view(one, *which)
+
+        def pass_on(block, part=everything, which=(0, views)):
             def one(view):
                 mine = partial(view, block, part)
                 hand(view, block, part).wait_recv()
@@ -343,7 +375,7 @@
                 store(outgoing, block, view, part, merged)
                 send(view, block, part).start()
 
-            each_view(one)
+            each_view(one, *which)
 
         def begin():
             with jax.named_scope("barrier"):
@@ -352,12 +384,15 @@
                 pair_copy().start()
             else:
                 peer_copy().start()
+                (slab_copy if lower else slab_end_copy)().start()
 
             @pl.when(below)
             def _():
                 down_copy(1).start()
                 if outer:
                     edge_copy(1).start()
+                if at == 1:
+                    slab_edge_copy(1).start()
 
             @pl.when(above)
             def _():
@@ -373,11 +408,11 @@
 
             @pl.when(jnp.logical_not(above))
             def _():
-                volume[:, :LEAD] = jnp.zeros((planes + 4, LEAD, cols), jnp.float32)
+                volume[:, :LEAD] = jnp.zeros((2 * planes + 3, LEAD, cols), jnp.float32)
 
             @pl.when(jnp.logical_not(below))
             def _():
-                volume[:, end : end + border] = jnp.zeros((planes + 4, border, cols), jnp.float32)
+                volume[:, end : end + border] = jnp.zeros((2 * planes + 3, border, cols), jnp.float32)
 
         def top_landed():
             @pl.when(above)
@@ -410,6 +445,7 @@
             begin()
             with jax.named_scope("hand2"):
                 hand_over(2)
+            pair_rest().start()
             top_landed()
             bottom_landed()
             shade_box(low, high, rows - LEAD, rows + extra)
@@ -418,20 +454,49 @@
             shade_box(low, high, 0, LEAD)
             with jax.named_scope("mate"):
                 send_mate()
+            with jax.named_scope("w_slab"):
+                slab_copy().wait_recv()
+
+                @pl.when(above)
+                def _():
+                    slab_edge_copy(-1).wait_recv()
+
+                slab_end_copy().wait_recv()
+            shade_box(high, span_high, 0, -(-(share + span_reach) // 8) * 8)
             keep_own()
         elif at == 3:
             begin()
             shade_box(low, high, LEAD, rows - LEAD)
             with jax.named_scope("hand0b"):
                 hand_over(0, halves[0])
-            top_landed()
-            shade_box(low, high, 0, LEAD)
-            with jax.named_scope("hand0a"):
-                hand_over(0, halves[1])
-            bottom_landed()
-            shade_box(low, high, rows - LEAD, rows)
-            with jax.named_scope("hand1"):
-                hand_over(1)
+            pair_rest().start()
+            def early():
+                top_landed()
+                shade_box(low, high, 0, LEAD)
+                with jax.named_scope("hand0a"):
+                    hand_over(0, halves[1])
+
+            def late(which):
+                with jax.named_scope("hand1"):
+                    hand_over(1, everything, which)
+
+            def bottom():
+                bottom_landed()
+                shade_box(low, high, rows - LEAD, rows)
+
+            @pl.when(distant)
+            def _():
+                bottom()
+                late(some)
+                early()
+                late(rest)
+
+            @pl.when(jnp.logical_not(distant))
+            def _():
+                early()
+                bottom()
+                late((0, views))
+
             shade_box(low, high, rows, rows + extra)
             with jax.named_scope("mate"):
                 send_mate()
@@ -451,11 +516,20 @@
             shade_box(far_edge, far_edge + 1, 0, rows)
             with jax.named_scope("w_pair"):
                 pair_copy().wait_recv()
-            shade_box(seam, seam + 2, LEAD, rows - LEAD)
+            if lower:
+                shade_box(seam, seam + 2, share + LEAD, rows - LEAD)
+            else:
+                shade_box(seam, seam + 2, LEAD, rows - share - LEAD)
 
             def rim():
+                with jax.named_scope("w_rest"):
+                    pair_rest().wait_recv()
                 edge_landed()
-                shade_box(seam, seam + 2, 0, LEAD)
+                if lower:
+                    shade_box(seam, seam + 2, 0, share + LEAD)
+                else:
+                    shade_box(seam, seam + 2, 0, LEAD)
+                    shade_box(seam, seam + 2, rows - share - LEAD, rows - LEAD)
 
             def fringe():
                 corners_landed()
@@ -463,11 +537,9 @@
                 shade_box(far_edge, far_edge + 1, rows, rows + extra)
 
             if lower:
-                rim()
-                with jax.named_scope("mate"):
-                    send_mate()
                 with jax.named_scope("pass2"):
                     pass_on(2)
+                rim()
                 fringe()
                 with jax.named_scope("pass3"):
                     pass_on(3)
@@ -478,18 +550,32 @@
                 fringe()
                 with jax.named_scope("mate"):
                     send_mate()
-                with jax.named_scope("pass0a"):
-                    pass_on(0, halves[1])
-                with jax.named_scope("pass1"):
-                    pass_on(1)
+
+                @pl.when(distant)
+                def _():
+                    pass_on(1, everything, some)
+                    with jax.named_scope("pass0a"):
+                        pass_on(0, halves[1])
+                    with jax.named_scope("pass1"):
+                        pass_on(1, everything, rest)
+
+                @pl.when(jnp.logical_not(distant))
+                def _():
+                    with jax.named_scope("pass0a"):
+                        pass_on(0, halves[1])
+                    with jax.named_scope("pass1"):
+                        pass_on(1)
+
             keep_own()
 
         def finish(view):
             swap = reverse[view] == 1
-            with jax.named_scope("w_mate"):
-                receive(view, mate).wait_recv()
-            mine, theirs = (load(incoming, source, view, everything) for source in (at, mate))
-            near = over(mine, theirs, swap) if at < mate else over(theirs, mine, swap)
+            near = load(incoming, at, view, everything)
+            if at != 0:
+                with jax.named_scope("w_mate"):
+                    receive(view, mate).wait_recv()
+                theirs = load(incoming, mate, view, everything)
+                near = over(near, theirs, swap) if at < mate else over(theirs, near, swap)
             with jax.named_scope("w_other"):
                 receive(view, other).wait_recv()
             far = load(incoming, other, view, everything)
@@ -502,14 +588,18 @@
 
         if outer:
             pair_copy().wait_send()
+            pair_rest().wait_send()
         else:
             peer_copy().wait_send()
+            (slab_copy if lower else slab_end_copy)().wait_send()
 
         @pl.when(below)
         def _():
             down_copy(1).wait_send()
             if outer:
                 edge_copy(1).wait_send()
+            if at == 1:
+                slab_edge_copy(1).wait_send()
 
         @pl.when(above)
         def _():
@@ -519,7 +609,7 @@
             else:
                 peer_corner(-1, peer_border).wait_send()
 
-        gone = pl.ds(0, groups - 1)
+        gone = pl.ds(0, groups - 2 if at == 1 else groups - 1)
         copy_to(outgoing.at[gone], handed.at[gone], images, hand_sem.at[0], (mate, h)).wait_send()
 
     for at in range(groups):
@@ -905,13 +995,13 @@
         out_specs=pl.BlockSpec(memory_space=pltpu.VMEM),
         scratch_shapes=[pltpu.SMEM(scalar.shape, scalar.dtype) for scalar in (light, gain, bias, shear, reverse)]
         + [
-            pltpu.VMEM((planes + 4, LEAD + rows + rows // 2 + LEAD, cols), jnp.float32),
-            pltpu.VMEM((4, planes + 4, rows + rows // 2, cols), jnp.float32),
+            pltpu.VMEM((2 * planes + 3, LEAD + rows + rows // 2 + LEAD, cols), jnp.float32),
+            pltpu.VMEM((4, 2 * planes + 2, rows + rows // 2, cols), jnp.float32),
             images,
             images,
             images,
-            pltpu.SemaphoreType.DMA((6,)),
             pltpu.SemaphoreType.DMA((7,)),
+            pltpu.SemaphoreType.DMA((8,)),
             pltpu.SemaphoreType.DMA((3 * views,)),
             pltpu.SemaphoreType.DMA((2 * views,)),
         ],

time: 16.8 us -> 16.5 us (0.982)
  the two profiles are of different devices: /device:TPU:0 before, /device:TPU:12 now
where the time goes in v2:
time: 16.5 us; the launch traced here: 16.4 us
  Pallas kernels  15.7 us (95%)
  local copies, waits for them, and re-layouts  0.66 us (4%)
    pallas_call x1, Pallas kernels, line(): pl.pallas_call(functools.partial(line_kernel, towers), name='render', out...  15.7 us
    unnamed x1, local copies, waits for them, and re-layouts  0.66 us

profile of v2, /device:TPU:12, one launch (start us, length us, event | category | flops | bytes accessed | tf_op | source)
XLA Modules:
  0.0 16.4 jit_solution(7107101243451664020)
XLA Ops:
  0.0 15.7 %render.1 = f32[4,4,16,128]{3,2,1,0:T(8,128)S(1)} custom-call(f32[8,64,128]{2,1,0:T(8,128)} %density.1, f32[3]{0:T(128)} %light_in.1, f32[3]{0:T(128)} %gain_in.1, f32[3]{0:T(128)} %bias_in.1, s32[4]{0:T(128)} %shear_in.1, s32[4]{0:T(128)} %reverse_in.1), custom_call_target="tpu_custom_call" | custom-call | tf_op jit(solution)/shard_map/render/pallas_call | solution.py:990
  15.7 0.7 %copy.8 = f32[4,4,16,128]{3,2,1,0:T(8,128)} copy(f32[4,4,16,128]{3,2,1,0:T(8,128)S(1)} %render.1) | data formatting | bytes 262144

commit v3 on v2

--- a/solution.py
+++ b/solution.py
@@ -40,6 +40,7 @@
     halo_sem,
     hand_sem,
     part_sem,
+    go_sem,
 ):
     planes, rows, cols = density.shape
     margin = rows // 2
@@ -53,7 +54,7 @@
     above, below = (h - 1 >= 0) & (h - 1 < towers), (h + 1 >= 0) & (h + 1 < towers)
     end = LEAD + rows
     own_planes = pl.ds(2, planes)
-    images, plane_sent, edge_sent, down_sent, up_sent, corner_sent, rest_sent = range(7)
+    images, plane_sent, edge_sent, down_sent, up_sent, corner_sent, rest_sent, relay_sent = range(8)
     slab_sent, slab_edge_sent = edge_sent, rest_sent
     pair_in, peer_in, edge_in, down_in, up_in, pair_corner_in, peer_corner_in, rest_in = range(8)
     slab_in, slab_edge_in, slab_end_in = pair_in, edge_in, peer_in
@@ -81,31 +82,39 @@
 
     barrier = pltpu.get_barrier_semaphore()
     expected = jnp.int32(0)
-    beside = [(1, 0), (-1, 0), (0, 1), (0, -1)]
-    greets = {at: list(beside) for at in range(groups)}
-    awaits = {at: list(beside) for at in range(groups)}
-    for at in (1, 2):
-        mate, peer = at ^ 1, 3 - at
+    greets = {at: [] for at in range(groups)}
+    awaits = {at: [] for at in range(groups)}
+
+    def greet(at, step_d, step_h, parity=None):
+        greets[at].append((step_d, step_h, parity))
+        awaits[at + step_d].append((-step_d, -step_h, parity if parity is None else (parity + step_h) % 2))
+
+    for at in range(groups):
+        mate = (at ^ 1) - at
+        outer = at in (0, 3)
         for step_h in (1, -1):
-            greets[at].append((mate - at, step_h))
-            awaits[mate].append((at - mate, -step_h))
-        greets[at].append((peer - at, 1))
-        awaits[peer].append((at - peer, -1))
-    for at, *step in ((0, 1, -1), (0, 2, 0)):
-        greets[at].append(tuple(step))
-        awaits[at + step[0]].append((-step[0], -step[1]))
+            greet(at, mate if outer else 0, step_h)
+            greet(at, 0 if outer else mate, step_h, 0)
+        greet(at, mate, 0)
+        if not outer:
+            greet(at, -mate, 0)
+            greet(at, -mate, 1)
+    greet(0, 2, 0)
+
+    def meets(at, step_d, step_h, parity):
+        ok = (d == at) & valid(step_d, step_h)
+        return ok if parity is None else ok & (lax.rem(h, 2) == parity)
+
     for at in range(groups):
 
-        for step in greets[at]:
-
-            @pl.when((d == at) & valid(*step))
-            def _(step=step):
-                pl.semaphore_signal(
-                    barrier, inc=1, device_id=(d + step[0], h + step[1]), device_id_type=MESH
-                )
+        for step_d, step_h, parity in greets[at]:
+
+            @pl.when(meets(at, step_d, step_h, parity))
+            def _(target=(d + step_d, h + step_h)):
+                pl.semaphore_signal(barrier, inc=1, device_id=target, device_id_type=MESH)
 
         for step in awaits[at]:
-            expected = expected + jnp.where((d == at) & valid(*step), 1, 0)
+            expected = expected + jnp.where(meets(at, *step), 1, 0)
 
     for scalar in scalars:
         scalar.wait()
@@ -116,7 +125,7 @@
     half_bias = [0.5 * bias[c] for c in range(3)]
     inside = jnp.where(below, 1.0, 0.0)
 
-    def shade(plane, row, count, keep):
+    def shade(plane, row, count, keep, loose=False):
         at = LEAD + row
         centre = volume[plane, at : at + count]
         lane = lax.broadcasted_iota(jnp.int32, (count, cols), 1)
@@ -124,7 +133,8 @@
         previous = jnp.where(lane == 0, 0.0, pltpu.roll(centre, 1, 1))
         dx = following - previous
         dz = volume[plane + 1, at : at + count] - volume[plane - 1, at : at + count]
-        dy = volume[plane, at + 1 : at + 1 + count] - volume[plane, at - 1 : at - 1 + count]
+        below_it = pltpu.roll(centre, count - 1, 0) if loose else volume[plane, at + 1 : at + 1 + count]
+        dy = below_it - volume[plane, at - 1 : at - 1 + count]
         facing = (lz * dz + ly * dy + lx * dx) * lax.rsqrt(4.0 + dz * dz + dy * dy + dx * dx)
         shading = 0.25 + 1.5 * jnp.maximum(facing, 0.0)
         optical = extinction * (
@@ -139,7 +149,7 @@
             fields[c, plane, to] = lit + lit * jnp.tanh(half_gain[c] * centre + half_bias[c])
         fields[3, plane, to] = opacity
 
-    def shade_box(low, high, top, bottom):
+    def shade_box(low, high, top, bottom, loose=False):
         tiles = (bottom - top) // 8
         together = max(1, min(high - low, -(-TOGETHER // tiles)))
         looped = (high - low) // together if high - low > together else 0
@@ -147,7 +157,7 @@
         def some(plane, count):
             for step in range(count):
                 for row, size in spans(top, min(bottom, rows), 16):
-                    shade(plane + step, row, size, None)
+                    shade(plane + step, row, size, None, loose)
                 for row, size in spans(max(top, rows), bottom, 16):
                     shade(plane + step, row, size, inside)
 
@@ -179,8 +189,10 @@
         return [f + clear * b for f, b in zip(front, behind)]
 
     everything = (0, share)
-    distant = (lax.rem(h, max(towers // 2, 1)) == 0) & (h > 0)
-    some, rest = (0, views // 2), (views // 2, views)
+    odd = lax.rem(h, 2) == 1
+    distant = (lax.rem(h, 2) == 0) & (h > 0)
+    ahead = jnp.where(h == towers // 2, views // 2, 1)
+    some, rest = (0, ahead), (ahead, views)
 
     def load(ref, block, view, part):
         return [ref[block, view, c, pl.ds(*part)] for c in range(4)]
@@ -235,7 +247,6 @@
         own_peer = pl.ds(planes + 1, 1) if lower else pl.ds(2, 1)
         peer_target = pl.ds(1, 1) if lower else pl.ds(planes + 2, 1)
         peer_border = extent(peer)[3] if peer else None
-        pair_border = extent(mate)[3] if outer else border
         whole = (LEAD, rows)
 
         cut = rows - share
@@ -250,9 +261,9 @@
         def peer_copy():
             return plane_copy(own_peer, peer_target, whole, whole, plane_sent, peer_in, (peer, h))
 
-        def pair_corner(step):
-            take, put = (LEAD, pair_border), (end, pair_border)
-            return plane_copy(own_pair, mate_pair, take, put, corner_sent, pair_corner_in, (d + mate - at, h + step))
+        def pair_relay(step):
+            take, put = (LEAD, border), (end, border)
+            return plane_copy(mate_pair, mate_pair, take, put, relay_sent, pair_corner_in, (d, h + step))
 
         def peer_corner(step, count):
             take, put = (LEAD, count), (end, count)
@@ -377,14 +388,32 @@
 
             each_view(one, *which)
 
+        def images_gone(blocks):
+            gone = pl.ds(0, blocks)
+            copy_to(outgoing.at[gone], handed.at[gone], images, hand_sem.at[0], (mate, h)).wait_send()
+
         def begin():
             with jax.named_scope("barrier"):
                 pl.semaphore_wait(barrier, expected)
             if outer:
                 pair_copy().start()
             else:
+
+                @pl.when(jnp.logical_not(odd))
+                def _():
+                    pl.semaphore_signal(go_sem, inc=1, device_id=(mate, h), device_id_type=MESH)
+
                 peer_copy().start()
                 (slab_copy if lower else slab_end_copy)().start()
+                columns()
+
+        def columns():
+            if outer:
+
+                @pl.when(jnp.logical_not(odd))
+                def _():
+                    with jax.named_scope("w_go"):
+                        pl.semaphore_wait(go_sem, 1)
 
             @pl.when(below)
             def _():
@@ -396,9 +425,7 @@
 
             @pl.when(above)
             def _():
-                if outer:
-                    pair_corner(-1).start()
-                else:
+                if not outer:
                     peer_corner(-1, peer_border).start()
                 up_copy(-1).start()
 
@@ -431,7 +458,7 @@
             def _():
                 with jax.named_scope("w_corner"):
                     peer_corner(1, border).wait_recv()
-                    pair_corner(1).wait_recv()
+                    pair_relay(1).wait_recv()
 
         def edge_landed():
             @pl.when(above)
@@ -446,6 +473,7 @@
             with jax.named_scope("hand2"):
                 hand_over(2)
             pair_rest().start()
+            columns()
             top_landed()
             bottom_landed()
             shade_box(low, high, rows - LEAD, rows + extra)
@@ -470,6 +498,9 @@
             with jax.named_scope("hand0b"):
                 hand_over(0, halves[0])
             pair_rest().start()
+            columns()
+            shade_box(low, high, rows - LEAD, rows, True)
+
             def early():
                 top_landed()
                 shade_box(low, high, 0, LEAD)
@@ -480,23 +511,24 @@
                 with jax.named_scope("hand1"):
                     hand_over(1, everything, which)
 
-            def bottom():
-                bottom_landed()
-                shade_box(low, high, rows - LEAD, rows)
-
             @pl.when(distant)
             def _():
-                bottom()
                 late(some)
                 early()
                 late(rest)
 
-            @pl.when(jnp.logical_not(distant))
+            @pl.when(h == 0)
             def _():
                 early()
-                bottom()
                 late((0, views))
 
+            @pl.when(odd)
+            def _():
+                early()
+                late((0, views))
+
+            bottom_landed()
+            shade_box(low, high, rows - LEAD, rows)
             shade_box(low, high, rows, rows + extra)
             with jax.named_scope("mate"):
                 send_mate()
@@ -507,62 +539,82 @@
             far_edge = planes + 1 if lower else 2
             seam = min(2 if lower else planes + 1, edge)
 
-            top_landed()
-            shade_box(3, planes + 1, 0, LEAD)
-            bottom_landed()
-            shade_box(3, planes + 1, rows - LEAD, rows + extra)
+
+            def top():
+                top_landed()
+                edge_landed()
+                shade_box(low, high, 0, LEAD)
+
+            def relay():
+                @pl.when(above)
+                def _():
+                    pair_relay(-1).start()
+
+            def rest_landed():
+                with jax.named_scope("w_rest"):
+                    pair_rest().wait_recv()
+                if lower:
+                    relay()
+                    shade_box(seam, seam + 2, LEAD, share + LEAD)
+                else:
+                    shade_box(seam, seam + 2, rows - share - LEAD, rows - LEAD)
+
+            def bottom():
+                bottom_landed()
+                corners_landed()
+                shade_box(low, high, rows - LEAD, rows + extra)
+
             with jax.named_scope("w_peer"):
                 peer_copy().wait_recv()
-            shade_box(far_edge, far_edge + 1, 0, rows)
+            shade_box(far_edge, far_edge + 1, LEAD, rows - LEAD)
+            if lower:
+                shade_box(3, planes + 2, rows - LEAD, rows, True)
             with jax.named_scope("w_pair"):
                 pair_copy().wait_recv()
             if lower:
                 shade_box(seam, seam + 2, share + LEAD, rows - LEAD)
-            else:
-                shade_box(seam, seam + 2, LEAD, rows - share - LEAD)
-
-            def rim():
-                with jax.named_scope("w_rest"):
-                    pair_rest().wait_recv()
-                edge_landed()
-                if lower:
-                    shade_box(seam, seam + 2, 0, share + LEAD)
-                else:
-                    shade_box(seam, seam + 2, 0, LEAD)
-                    shade_box(seam, seam + 2, rows - share - LEAD, rows - LEAD)
-
-            def fringe():
-                corners_landed()
-                shade_box(seam, seam + 2, rows - LEAD, rows + extra)
-                shade_box(far_edge, far_edge + 1, rows, rows + extra)
-
-            if lower:
                 with jax.named_scope("pass2"):
                     pass_on(2)
-                rim()
-                fringe()
+                rest_landed()
+                top()
+                bottom()
                 with jax.named_scope("pass3"):
                     pass_on(3)
             else:
+                relay()
+                shade_box(seam, seam + 2, LEAD, rows - share - LEAD)
                 with jax.named_scope("pass0b"):
                     pass_on(0, halves[0])
-                rim()
-                fringe()
-                with jax.named_scope("mate"):
-                    send_mate()
+                rest_landed()
+
+                def mate_part():
+                    bottom()
+                    with jax.named_scope("mate"):
+                        send_mate()
+
+                def early():
+                    top()
+                    with jax.named_scope("pass0a"):
+                        pass_on(0, halves[1])
 
                 @pl.when(distant)
                 def _():
-                    pass_on(1, everything, some)
-                    with jax.named_scope("pass0a"):
-                        pass_on(0, halves[1])
+                    mate_part()
                     with jax.named_scope("pass1"):
-                        pass_on(1, everything, rest)
-
-                @pl.when(jnp.logical_not(distant))
+                        pass_on(1, everything, some)
+                    early()
+                    pass_on(1, everything, rest)
+
+                @pl.when(h == 0)
                 def _():
-                    with jax.named_scope("pass0a"):
-                        pass_on(0, halves[1])
+                    mate_part()
+                    early()
+                    pass_on(1)
+
+                @pl.when(odd)
+                def _():
+                    early()
+                    mate_part()
                     with jax.named_scope("pass1"):
                         pass_on(1)
 
@@ -604,14 +656,11 @@
         @pl.when(above)
         def _():
             up_copy(-1).wait_send()
-            if outer:
-                pair_corner(-1).wait_send()
-            else:
+            if not outer:
                 peer_corner(-1, peer_border).wait_send()
-
-        gone = pl.ds(0, groups - 2 if at == 1 else groups - 1)
-        copy_to(outgoing.at[gone], handed.at[gone], images, hand_sem.at[0], (mate, h)).wait_send()
-
+                pair_relay(-1).wait_send()
+
+        images_gone(2 if at == 1 else 3)
     for at in range(groups):
 
         @pl.when(d == at)
@@ -1000,10 +1049,11 @@
             images,
             images,
             images,
-            pltpu.SemaphoreType.DMA((7,)),
+            pltpu.SemaphoreType.DMA((8,)),
             pltpu.SemaphoreType.DMA((8,)),
             pltpu.SemaphoreType.DMA((3 * views,)),
             pltpu.SemaphoreType.DMA((2 * views,)),
+            pltpu.SemaphoreType.REGULAR,
         ],
         compiler_params=pltpu.CompilerParams(collective_id=0, has_side_effects=True, vmem_limit_bytes=60 * 1024 * 1024),
     )(density, light, gain, bias, shear, reverse)

time: 16.5 us -> 16.3 us (0.988)
  the two profiles are of different devices: /device:TPU:12 before, /device:TPU:25 now
where the time goes in v3:
time: 16.3 us; the launch traced here: 16.2 us
  Pallas kernels  15.5 us (95%)
  local copies, waits for them, and re-layouts  0.66 us (4%)
    pallas_call x1, Pallas kernels, line(): pl.pallas_call(functools.partial(line_kernel, towers), name='render', out...  15.5 us
    unnamed x1, local copies, waits for them, and re-layouts  0.66 us

profile of v3, /device:TPU:25, one launch (start us, length us, event | category | flops | bytes accessed | tf_op | source)
XLA Modules:
  0.0 16.2 jit_solution(15626050436808671220)
XLA Ops:
  0.0 15.5 %render.1 = f32[4,4,16,128]{3,2,1,0:T(8,128)S(1)} custom-call(f32[8,64,128]{2,1,0:T(8,128)} %density.1, f32[3]{0:T(128)} %light_in.1, f32[3]{0:T(128)} %gain_in.1, f32[3]{0:T(128)} %bias_in.1, s32[4]{0:T(128)} %shear_in.1, s32[4]{0:T(128)} %reverse_in.1), custom_call_target="tpu_custom_call" | custom-call | tf_op jit(solution)/shard_map/render/pallas_call | solution.py:1039
  15.5 0.7 %copy.8 = f32[4,4,16,128]{3,2,1,0:T(8,128)} copy(f32[4,4,16,128]{3,2,1,0:T(8,128)S(1)} %render.1) | data formatting | bytes 262144

commit v4 on v3

--- a/solution.py
+++ b/solution.py
@@ -54,15 +54,17 @@
     above, below = (h - 1 >= 0) & (h - 1 < towers), (h + 1 >= 0) & (h + 1 < towers)
     end = LEAD + rows
     own_planes = pl.ds(2, planes)
-    images, plane_sent, edge_sent, down_sent, up_sent, corner_sent, rest_sent, relay_sent = range(8)
-    slab_sent, slab_edge_sent = edge_sent, rest_sent
+    images, plane_sent, edge_sent, down_sent, up_sent, corner_sent, rest_sent, relay_sent, flank_edge_sent, flank_end_sent = range(10)
+    slab_sent, slab_edge_sent, flank_sent = edge_sent, rest_sent, rest_sent
     pair_in, peer_in, edge_in, down_in, up_in, pair_corner_in, peer_corner_in, rest_in = range(8)
     slab_in, slab_edge_in, slab_end_in = pair_in, edge_in, peer_in
+    flank_in, flank_edge_in, flank_end_in = pair_in, edge_in, peer_in
 
     own = pltpu.make_async_copy(
         density, volume.at[own_planes, pl.ds(LEAD, rows)], sent_sem.at[images]
     )
     own.start()
+
     scalars = [
         pltpu.make_async_copy(source, target, sent_sem.at[1 + index])
         for index, (source, target) in enumerate(
@@ -291,6 +293,24 @@
             take = (LEAD, span_rows)
             return plane_copy(pl.ds(2, 1), slab_end, take, take, slab_sent, slab_end_in, (0 if at else 2, h))
 
+        flank = planes + 4
+        flank_top = rows - share - LEAD
+        flank_reach = (3 * planes - 1) * margin // total_planes
+        flank_rows = min(extent(2)[3], -(-(flank_reach + 1) // 8) * 8)
+        flank_planes = pl.ds(flank, planes)
+
+        def flank_copy():
+            take = (LEAD + flank_top, share + LEAD)
+            return plane_copy(own_planes, flank_planes, take, take, flank_sent, flank_in, (3 if at == 2 else 2, h))
+
+        def flank_edge_copy(step):
+            take, put = (LEAD, flank_rows), (end, flank_rows)
+            return plane_copy(own_planes, flank_planes, take, put, flank_edge_sent, flank_edge_in, (d + (1 if at == 2 else -1), h + step))
+
+        def flank_end_copy():
+            take = (LEAD + flank_top, share + LEAD + flank_rows)
+            return plane_copy(pl.ds(1, 1), pl.ds(flank - 1, 1), take, take, flank_end_sent, flank_end_in, (3 if at == 2 else 2, h))
+
         def down_copy(step):
             return copy_to(
                 volume.at[own_planes, pl.ds(rows, LEAD)],
@@ -339,18 +359,22 @@
                 (source, h),
             )
 
-        def partial(view, block, part, high=high, reach=reach):
+        def partial(view, block, part, span=None):
             step = shear[view]
             backward = reverse[view]
-            count = high - low
+            count = high - low if span is None else 2 * planes
             size = part[1]
             colour = [jnp.zeros((size, cols), jnp.float32) for _ in range(3)]
             clear = jnp.ones((size, cols), jnp.float32)
             covered = jnp.zeros((size, cols), jnp.float32)
             for i in range(count):
-                plane = jnp.where(backward == 1, low + count - 1 - i, low + i)
-                offset = lax.div((first + plane) * step, jnp.int32(total_planes))
-                offset = jnp.minimum(jnp.maximum(offset, 0), reach)
+                index = jnp.where(backward == 1, count - 1 - i, i)
+                if span is None:
+                    plane, depth, limit = low + index, first + low + index, reach
+                else:
+                    plane, depth, limit = span(index)
+                offset = lax.div(depth * step, jnp.int32(total_planes))
+                offset = jnp.minimum(jnp.maximum(offset, 0), limit)
                 rows_at = pl.ds(offset + block * share + part[0], size)
                 for c in range(3):
                     colour[c] = colour[c] + clear * fields[c, plane, rows_at]
@@ -366,8 +390,14 @@
             each_view(one)
 
         def keep_own():
-            span = (span_high, span_reach) if at == 0 else (high, reach)
-            each_view(lambda view: store(incoming, at, view, everything, partial(view, at, everything, *span)))
+            def front_pair(index):
+                return 2 + index, index, span_reach
+
+            def back_pair(index):
+                return jnp.where(index < planes, flank + index, index - planes + 2), 2 * planes + index, reach
+
+            span = {0: front_pair, 3: back_pair}.get(at)
+            each_view(lambda view: store(incoming, at, view, everything, partial(view, at, everything, span)))
 
         def hand_over(block, part=everything, which=(0, views)):
             def one(view):
@@ -397,6 +427,8 @@
                 pl.semaphore_wait(barrier, expected)
             if outer:
                 pair_copy().start()
+                if lower:
+                    pair_rest().start()
             else:
 
                 @pl.when(jnp.logical_not(odd))
@@ -405,6 +437,8 @@
 
                 peer_copy().start()
                 (slab_copy if lower else slab_end_copy)().start()
+                if not lower:
+                    flank_copy().start()
                 columns()
 
         def columns():
@@ -427,6 +461,8 @@
             def _():
                 if not outer:
                     peer_corner(-1, peer_border).start()
+                if at == 2:
+                    flank_edge_copy(-1).start()
                 up_copy(-1).start()
 
         def blank():
@@ -435,11 +471,11 @@
 
             @pl.when(jnp.logical_not(above))
             def _():
-                volume[:, :LEAD] = jnp.zeros((2 * planes + 3, LEAD, cols), jnp.float32)
+                volume[:, :LEAD] = jnp.zeros((2 * planes + 5, LEAD, cols), jnp.float32)
 
             @pl.when(jnp.logical_not(below))
             def _():
-                volume[:, end : end + border] = jnp.zeros((2 * planes + 3, border, cols), jnp.float32)
+                volume[:, end : end + border] = jnp.zeros((2 * planes + 5, border, cols), jnp.float32)
 
         def top_landed():
             @pl.when(above)
@@ -453,11 +489,16 @@
                 with jax.named_scope("w_up"):
                     up_copy(1).wait_recv()
 
-        def corners_landed():
+        def peer_corner_landed():
             @pl.when(below)
             def _():
+                with jax.named_scope("w_pcorner"):
+                    peer_corner(1, border).wait_recv()
+
+        def pair_corner_landed():
+            @pl.when(below)
+            def _():
                 with jax.named_scope("w_corner"):
-                    peer_corner(1, border).wait_recv()
                     pair_relay(1).wait_recv()
 
         def edge_landed():
@@ -472,7 +513,6 @@
             begin()
             with jax.named_scope("hand2"):
                 hand_over(2)
-            pair_rest().start()
             columns()
             top_landed()
             bottom_landed()
@@ -532,6 +572,20 @@
             shade_box(low, high, rows, rows + extra)
             with jax.named_scope("mate"):
                 send_mate()
+            with jax.named_scope("w_flank"):
+                flank_copy().wait_recv()
+
+                @pl.when(below)
+                def _():
+                    flank_edge_copy(1).wait_recv()
+
+                flank_end_copy().wait_recv()
+            top_row, bottom_row = rows - share, rows + flank_rows
+            there = pl.ds(LEAD + top_row, bottom_row - top_row)
+            volume[1, there] = volume[flank + planes - 1, there]
+            volume[flank + planes, there] = volume[2, there]
+            shade_box(flank, flank + planes, top_row, bottom_row)
+            shade_box(2, 3, top_row, bottom_row)
             keep_own()
         else:
             shade_box(3, planes + 1, LEAD, rows - LEAD)
@@ -561,7 +615,9 @@
 
             def bottom():
                 bottom_landed()
-                corners_landed()
+                pair_corner_landed()
+                if lower:
+                    peer_corner_landed()
                 shade_box(low, high, rows - LEAD, rows + extra)
 
             with jax.named_scope("w_peer"):
@@ -573,9 +629,9 @@
                 pair_copy().wait_recv()
             if lower:
                 shade_box(seam, seam + 2, share + LEAD, rows - LEAD)
+                rest_landed()
                 with jax.named_scope("pass2"):
                     pass_on(2)
-                rest_landed()
                 top()
                 bottom()
                 with jax.named_scope("pass3"):
@@ -585,12 +641,9 @@
                 shade_box(seam, seam + 2, LEAD, rows - share - LEAD)
                 with jax.named_scope("pass0b"):
                     pass_on(0, halves[0])
+                peer_corner_landed()
+                flank_end_copy().start()
                 rest_landed()
-
-                def mate_part():
-                    bottom()
-                    with jax.named_scope("mate"):
-                        send_mate()
 
                 def early():
                     top()
@@ -599,31 +652,24 @@
 
                 @pl.when(distant)
                 def _():
-                    mate_part()
                     with jax.named_scope("pass1"):
                         pass_on(1, everything, some)
                     early()
                     pass_on(1, everything, rest)
 
-                @pl.when(h == 0)
-                def _():
-                    mate_part()
-                    early()
-                    pass_on(1)
-
-                @pl.when(odd)
+                @pl.when(jnp.logical_not(distant))
                 def _():
                     early()
-                    mate_part()
                     with jax.named_scope("pass1"):
                         pass_on(1)
 
+                bottom()
             keep_own()
 
         def finish(view):
             swap = reverse[view] == 1
             near = load(incoming, at, view, everything)
-            if at != 0:
+            if not outer:
                 with jax.named_scope("w_mate"):
                     receive(view, mate).wait_recv()
                 theirs = load(incoming, mate, view, everything)
@@ -644,6 +690,9 @@
         else:
             peer_copy().wait_send()
             (slab_copy if lower else slab_end_copy)().wait_send()
+            if not lower:
+                flank_copy().wait_send()
+                flank_end_copy().wait_send()
 
         @pl.when(below)
         def _():
@@ -659,8 +708,10 @@
             if not outer:
                 peer_corner(-1, peer_border).wait_send()
                 pair_relay(-1).wait_send()
-
-        images_gone(2 if at == 1 else 3)
+            if at == 2:
+                flank_edge_copy(-1).wait_send()
+
+        images_gone(3 if outer else 2)
     for at in range(groups):
 
         @pl.when(d == at)
@@ -1044,12 +1095,12 @@
         out_specs=pl.BlockSpec(memory_space=pltpu.VMEM),
         scratch_shapes=[pltpu.SMEM(scalar.shape, scalar.dtype) for scalar in (light, gain, bias, shear, reverse)]
         + [
-            pltpu.VMEM((2 * planes + 3, LEAD + rows + rows // 2 + LEAD, cols), jnp.float32),
-            pltpu.VMEM((4, 2 * planes + 2, rows + rows // 2, cols), jnp.float32),
+            pltpu.VMEM((2 * planes + 5, LEAD + rows + rows // 2 + LEAD, cols), jnp.float32),
+            pltpu.VMEM((4, 2 * planes + 4, rows + rows // 2, cols), jnp.float32),
             images,
             images,
             images,
-            pltpu.SemaphoreType.DMA((8,)),
+            pltpu.SemaphoreType.DMA((10,)),
             pltpu.SemaphoreType.DMA((8,)),
             pltpu.SemaphoreType.DMA((3 * views,)),
             pltpu.SemaphoreType.DMA((2 * views,)),

time: 16.3 us -> 16 us (0.982)
  the two profiles are of different devices: /device:TPU:25 before, /device:TPU:12 now
where the time goes in v4:
time: 16 us; the launch traced here: 15.8 us
  Pallas kernels  15.2 us (95%)
  local copies, waits for them, and re-layouts  0.66 us (4%)
    pallas_call x1, Pallas kernels, line(): pl.pallas_call(functools.partial(line_kernel, towers), name='render', out...  15.2 us
    unnamed x1, local copies, waits for them, and re-layouts  0.66 us

profile of v4, /device:TPU:12, one launch (start us, length us, event | category | flops | bytes accessed | tf_op | source)
XLA Modules:
  0.0 15.8 jit_solution(5588742039174403904)
XLA Ops:
  0.0 15.2 %render.1 = f32[4,4,16,128]{3,2,1,0:T(8,128)S(1)} custom-call(f32[8,64,128]{2,1,0:T(8,128)} %density.1, f32[3]{0:T(128)} %light_in.1, f32[3]{0:T(128)} %gain_in.1, f32[3]{0:T(128)} %bias_in.1, s32[4]{0:T(128)} %shear_in.1, s32[4]{0:T(128)} %reverse_in.1), custom_call_target="tpu_custom_call" | custom-call | tf_op jit(solution)/shard_map/render/pallas_call | solution.py:1090
  15.2 0.7 %copy.8 = f32[4,4,16,128]{3,2,1,0:T(8,128)} copy(f32[4,4,16,128]{3,2,1,0:T(8,128)S(1)} %render.1) | data formatting | bytes 262144

commit v5 on v4

--- a/solution.py
+++ b/solution.py
@@ -60,13 +60,21 @@
     slab_in, slab_edge_in, slab_end_in = pair_in, edge_in, peer_in
     flank_in, flank_edge_in, flank_end_in = pair_in, edge_in, peer_in
 
-    own = pltpu.make_async_copy(
-        density, volume.at[own_planes, pl.ds(LEAD, rows)], sent_sem.at[images]
+    early_planes = jnp.where(d < groups // 2, planes - 2, 0)
+    later_planes = jnp.where(d < groups // 2, 0, 2)
+    own, own_rest = (
+        pltpu.make_async_copy(
+            density.at[pl.ds(start, count)],
+            volume.at[pl.ds(2 + start, count), pl.ds(LEAD, rows)],
+            sent_sem.at[index],
+        )
+        for start, count, index in ((early_planes, 2, images), (later_planes, planes - 2, relay_sent))
     )
     own.start()
+    own_rest.start()
 
     scalars = [
-        pltpu.make_async_copy(source, target, sent_sem.at[1 + index])
+        pltpu.make_async_copy(source, target, sent_sem.at[(edge_sent, down_sent, up_sent, corner_sent, rest_sent)[index]])
         for index, (source, target) in enumerate(
             zip((light_in, gain_in, bias_in, shear_in, reverse_in), (light, gain, bias, shear, reverse))
         )
@@ -118,9 +126,26 @@
         for step in awaits[at]:
             expected = expected + jnp.where(meets(at, *step), 1, 0)
 
+    own.wait()
+
+    @pl.when(d == groups - 1)
+    def _():
+        with jax.named_scope("barrier"):
+            pl.semaphore_wait(barrier, expected)
+        first_pair = volume.at[pl.ds(2, 2), pl.ds(LEAD, rows - share)]
+        first_target = volume.at[pl.ds(planes + 2, 2), pl.ds(LEAD, rows - share)]
+        pltpu.make_async_remote_copy(
+            src_ref=first_pair,
+            dst_ref=first_target,
+            send_sem=sent_sem.at[plane_sent],
+            recv_sem=halo_sem.at[pair_in],
+            device_id=(d - 1, h),
+            device_id_type=MESH,
+        ).start()
+
     for scalar in scalars:
         scalar.wait()
-    own.wait()
+    own_rest.wait()
 
     lz, ly, lx = light[0], light[1], light[2]
     half_gain = [0.5 * gain[c] for c in range(3)]
@@ -194,7 +219,7 @@
     odd = lax.rem(h, 2) == 1
     distant = (lax.rem(h, 2) == 0) & (h > 0)
     ahead = jnp.where(h == towers // 2, views // 2, 1)
-    some, rest = (0, ahead), (ahead, views)
+    some, rest = (0, ahead), (ahead, views - 1)
 
     def load(ref, block, view, part):
         return [ref[block, view, c, pl.ds(*part)] for c in range(4)]
@@ -330,7 +355,8 @@
             )
 
         def hand(view, block, part):
-            index = hand_at[block, part] * views + view
+            split = block == 1 and part in halves
+            index = 3 * views - 1 + halves.index(part) if split else hand_at[block, part] * views + view
             return copy_to(
                 outgoing.at[block, view, :, pl.ds(*part)],
                 handed.at[block, view, :, pl.ds(*part)],
@@ -423,6 +449,8 @@
             copy_to(outgoing.at[gone], handed.at[gone], images, hand_sem.at[0], (mate, h)).wait_send()
 
         def begin():
+            if at == 3:
+                return
             with jax.named_scope("barrier"):
                 pl.semaphore_wait(barrier, expected)
             if outer:
@@ -534,11 +562,12 @@
             keep_own()
         elif at == 3:
             begin()
+            pl.when(odd)(columns)
             shade_box(low, high, LEAD, rows - LEAD)
             with jax.named_scope("hand0b"):
                 hand_over(0, halves[0])
             pair_rest().start()
-            columns()
+            pl.when(jnp.logical_not(odd))(columns)
             shade_box(low, high, rows - LEAD, rows, True)
 
             def early():
@@ -551,21 +580,28 @@
                 with jax.named_scope("hand1"):
                     hand_over(1, everything, which)
 
+            def last():
+                for half in halves:
+                    hand_over(1, half, (views - 1, views))
+
             @pl.when(distant)
             def _():
                 late(some)
                 early()
                 late(rest)
+                last()
 
             @pl.when(h == 0)
             def _():
                 early()
-                late((0, views))
+                late((0, views - 1))
+                last()
 
             @pl.when(odd)
             def _():
                 early()
-                late((0, views))
+                late((0, views - 1))
+                last()
 
             bottom_landed()
             shade_box(low, high, rows - LEAD, rows)
@@ -645,6 +681,10 @@
                 flank_end_copy().start()
                 rest_landed()
 
+                def last():
+                    for half in halves:
+                        pass_on(1, half, (views - 1, views))
+
                 def early():
                     top()
                     with jax.named_scope("pass0a"):
@@ -656,12 +696,14 @@
                         pass_on(1, everything, some)
                     early()
                     pass_on(1, everything, rest)
+                    last()
 
                 @pl.when(jnp.logical_not(distant))
                 def _():
                     early()
                     with jax.named_scope("pass1"):
-                        pass_on(1)
+                        pass_on(1, everything, (0, views - 1))
+                        last()
 
                 bottom()
             keep_own()
@@ -1102,7 +1144,7 @@
             images,
             pltpu.SemaphoreType.DMA((10,)),
             pltpu.SemaphoreType.DMA((8,)),
-            pltpu.SemaphoreType.DMA((3 * views,)),
+            pltpu.SemaphoreType.DMA((3 * views + 1,)),
             pltpu.SemaphoreType.DMA((2 * views,)),
             pltpu.SemaphoreType.REGULAR,
         ],

time: 16 us -> 15.6 us (0.975)
  Pallas kernels: 15.2 us -> 14.8 us
    pallas_call x1, Pallas kernels: 15.2 us -> 14.8 us  [line(): pl.pallas_call(functools.partial(line_kernel, towers), name='render', out...]
where the time goes in v5:
time: 15.6 us; the launch traced here: 15.5 us
  Pallas kernels  14.8 us (95%)
  local copies, waits for them, and re-layouts  0.66 us (4%)
    pallas_call x1, Pallas kernels, line(): pl.pallas_call(functools.partial(line_kernel, towers), name='render', out...  14.8 us
    unnamed x1, local copies, waits for them, and re-layouts  0.66 us

profile of v5, /device:TPU:12, one launch (start us, length us, event | category | flops | bytes accessed | tf_op | source)
XLA Modules:
  0.0 15.5 jit_solution(10559736578929858337)
XLA Ops:
  0.0 14.8 %render.1 = f32[4,4,16,128]{3,2,1,0:T(8,128)S(1)} custom-call(f32[8,64,128]{2,1,0:T(8,128)} %density.1, f32[3]{0:T(128)} %light_in.1, f32[3]{0:T(128)} %gain_in.1, f32[3]{0:T(128)} %bias_in.1, s32[4]{0:T(128)} %shear_in.1, s32[4]{0:T(128)} %reverse_in.1), custom_call_target="tpu_custom_call" | custom-call | tf_op jit(solution)/shard_map/render/pallas_call | solution.py:1132
  14.8 0.7 %copy.8 = f32[4,4,16,128]{3,2,1,0:T(8,128)} copy(f32[4,4,16,128]{3,2,1,0:T(8,128)S(1)} %render.1) | data formatting | bytes 262144

commit v6 on v5

--- a/solution.py
+++ b/solution.py
@@ -366,24 +366,26 @@
             )
 
         def send(view, block, part):
-            slot = 0 if block == mate else views
+            slot = 0 if block == mate else 1 + view
             return copy_to(
                 outgoing.at[block, view, :, pl.ds(*part)],
                 incoming.at[at, view, :, pl.ds(*part)],
                 images,
-                part_sem.at[slot + view],
+                part_sem.at[slot],
                 (block, h),
             )
 
-        def receive(view, source):
-            slot = 0 if source == mate else views
+        def receive(view):
             return copy_to(
                 outgoing.at[at, view],
-                incoming.at[source, view],
+                incoming.at[other, view],
                 images,
-                part_sem.at[slot + view],
-                (source, h),
+                part_sem.at[1 + view],
+                (other, h),
             )
+
+        def receive_mate():
+            return copy_to(outgoing.at[at], incoming.at[mate], images, part_sem.at[0], (mate, h))
 
         def partial(view, block, part, span=None):
             step = shear[view]
@@ -712,16 +714,18 @@
             swap = reverse[view] == 1
             near = load(incoming, at, view, everything)
             if not outer:
-                with jax.named_scope("w_mate"):
-                    receive(view, mate).wait_recv()
                 theirs = load(incoming, mate, view, everything)
                 near = over(near, theirs, swap) if at < mate else over(theirs, near, swap)
             with jax.named_scope("w_other"):
-                receive(view, other).wait_recv()
+                receive(view).wait_recv()
             far = load(incoming, other, view, everything)
             total = over(near, far, swap) if lower else over(far, near, swap)
             for c in range(4):
                 out[c, view] = total[c]
+
+        if not outer:
+            with jax.named_scope("w_mate"):
+                receive_mate().wait_recv()
 
         for view in range(views):
             finish(view)
@@ -1145,7 +1149,7 @@
             pltpu.SemaphoreType.DMA((10,)),
             pltpu.SemaphoreType.DMA((8,)),
             pltpu.SemaphoreType.DMA((3 * views + 1,)),
-            pltpu.SemaphoreType.DMA((2 * views,)),
+            pltpu.SemaphoreType.DMA((1 + views,)),
             pltpu.SemaphoreType.REGULAR,
         ],
         compiler_params=pltpu.CompilerParams(collective_id=0, has_side_effects=True, vmem_limit_bytes=60 * 1024 * 1024),

time: 15.6 us -> 15.6 us (level)
  no operation moved by 1% of the time
where the time goes in v6:
time: 15.6 us; the launch traced here: 15.5 us
  Pallas kernels  14.8 us (95%)
  local copies, waits for them, and re-layouts  0.66 us (4%)
    pallas_call x1, Pallas kernels, line(): pl.pallas_call(functools.partial(line_kernel, towers), name='render', out...  14.8 us
    unnamed x1, local copies, waits for them, and re-layouts  0.66 us

profile of v6, /device:TPU:12, one launch (start us, length us, event | category | flops | bytes accessed | tf_op | source)
XLA Modules:
  0.0 15.5 jit_solution(12012883545791123466)
XLA Ops:
  0.0 14.8 %render.1 = f32[4,4,16,128]{3,2,1,0:T(8,128)S(1)} custom-call(f32[8,64,128]{2,1,0:T(8,128)} %density.1, f32[3]{0:T(128)} %light_in.1, f32[3]{0:T(128)} %gain_in.1, f32[3]{0:T(128)} %bias_in.1, s32[4]{0:T(128)} %shear_in.1, s32[4]{0:T(128)} %reverse_in.1), custom_call_target="tpu_custom_call" | custom-call | tf_op jit(solution)/shard_map/render/pallas_call | solution.py:1136
  14.8 0.7 %copy.8 = f32[4,4,16,128]{3,2,1,0:T(8,128)} copy(f32[4,4,16,128]{3,2,1,0:T(8,128)S(1)} %render.1) | data formatting | bytes 262144

commit v7 on v6

--- a/solution.py
+++ b/solution.py
@@ -608,6 +608,7 @@
             bottom_landed()
             shade_box(low, high, rows - LEAD, rows)
             shade_box(low, high, rows, rows + extra)
+            images_gone(2)
             with jax.named_scope("mate"):
                 send_mate()
             with jax.named_scope("w_flank"):
@@ -757,7 +758,7 @@
             if at == 2:
                 flank_edge_copy(-1).wait_send()
 
-        images_gone(3 if outer else 2)
+        images_gone({0: 3, 1: 2, 2: 2, 3: 1}[at])
     for at in range(groups):
 
         @pl.when(d == at)

time: 15.6 us -> 15.7 us (level)
  no operation moved by 1% of the time
where the time goes in v7:
time: 15.7 us; the launch traced here: 15.5 us
  Pallas kernels  14.8 us (94%)
  local copies, waits for them, and re-layouts  0.66 us (4%)
    pallas_call x1, Pallas kernels, line(): pl.pallas_call(functools.partial(line_kernel, towers), name='render', out...  14.8 us
    unnamed x1, local copies, waits for them, and re-layouts  0.66 us

profile of v7, /device:TPU:12, one launch (start us, length us, event | category | flops | bytes accessed | tf_op | source)
XLA Modules:
  0.0 15.5 jit_solution(7096313112438168640)
XLA Ops:
  0.0 14.8 %render.1 = f32[4,4,16,128]{3,2,1,0:T(8,128)S(1)} custom-call(f32[8,64,128]{2,1,0:T(8,128)} %density.1, f32[3]{0:T(128)} %light_in.1, f32[3]{0:T(128)} %gain_in.1, f32[3]{0:T(128)} %bias_in.1, s32[4]{0:T(128)} %shear_in.1, s32[4]{0:T(128)} %reverse_in.1), custom_call_target="tpu_custom_call" | custom-call | tf_op jit(solution)/shard_map/render/pallas_call | solution.py:1137
  14.8 0.7 %copy.8 = f32[4,4,16,128]{3,2,1,0:T(8,128)} copy(f32[4,4,16,128]{3,2,1,0:T(8,128)S(1)} %render.1) | data formatting | bytes 262144
